TPU v7x, 32 devices: a whole 2x2x4 slice. The times are simulated.
32 devices in a mesh: gx: 4 (over x, core), gy: 8 (over z, y).
Axes of the slice: x: 2, y: 2, z: 4, core: 2. Of those that a mesh axis runs over, the one named last changes fastest.
Arguments:
- velocity: float32 [3, 1024, 512], P(None, ('gx', 'gy')), may hold values from -6 to 6
- depart: float32 [3, 524288], P(None, ('gx', 'gy')), may hold values from -1 to 1
- owner_rank: int32 [524288, 1], P(('gx', 'gy')), may hold values from 0 to 31; in each aligned block of 16384 rows (0 to 16383, 16384 to 32767, ...) at most 1024 rows name the same one
- owner_element_index: int32 [524288], P(('gx', 'gy')), may hold values from 0 to 31
- neighbours: int32 [6, 1024], P(None, ('gx', 'gy')), may hold values from -1 to 1023, as said below
Outputs:
- advected: float32 [3, 1024, 512], P(None, ('gx', 'gy'))
Inputs may be any that keep to these rules, and one draw needn't show every extreme that they name: `owner_rank`: within the rows of one device no owner device is named by more than 1024 rows, and in some device's rows one owner is named exactly 1024 times. `neighbours`: -1 marks a boundary face; any other entry is an element of the same block of 32 consecutive elements as the entry's own element, or of the block just before or just after it.
All inputs are finite; a program needn't handle non-finite values.
Results may differ from a plain program's by a relative error of at most 0.0003.
Values sent between devices are 32-bit elements; how exact they have to be, the bound alone decides.
A program may use at most 64 MiB of HBM per device.

v0:
```python
import math

import jax
import jax.numpy as jnp
import numpy as np
from jax import lax
from jax.sharding import PartitionSpec as P

GLL_POINTS = np.array(
    [
        -1.0,
        -0.8717401485096066,
        -0.5917001814331423,
        -0.2092992179024789,
        0.2092992179024789,
        0.5917001814331423,
        0.8717401485096066,
        1.0,
    ]
)


def with_halo(cells, sides, width):
    for axis, dim in sides:
        count = lax.axis_size(axis)
        ends = count - 1
        head = lax.slice_in_dim(cells, 0, width, axis=dim)
        tail = lax.slice_in_dim(cells, cells.shape[dim] - width, cells.shape[dim], axis=dim)
        cells = jnp.concatenate(
            [
                lax.ppermute(tail, axis, [(i, (i + 1) % count) for i in range(ends)]),
                cells,
                lax.ppermute(head, axis, [((i + 1) % count, i) for i in range(ends)]),
            ],
            axis=dim,
        )
    return cells


def lagrange(coords):
    columns = []
    for node_id in range(8):
        factor = jnp.ones_like(coords)
        for other in range(8):
            if other != node_id:
                factor = factor * (
                    (coords - float(GLL_POINTS[other]))
                    / float(GLL_POINTS[node_id] - GLL_POINTS[other])
                )
        columns.append(factor)
    return jnp.stack(columns, axis=-1)


def face_slicer(face_id):
    whole_range = slice(None)
    edge_at = 7 * (face_id % 2)
    if face_id < 2:
        return (whole_range, whole_range, edge_at)
    if face_id < 4:
        return (whole_range, whole_range, whole_range, edge_at)
    return (whole_range, whole_range, whole_range, whole_range, edge_at)


def faces_of(nodal_cube):
    shape_lead = (nodal_cube.shape[0], nodal_cube.shape[1], 64)
    return jnp.stack(
        [nodal_cube[face_slicer(face_id)].reshape(shape_lead) for face_id in range(6)], axis=1
    )


def apply_faces_hot(nodal_cube, own_faces, neighbour_faces, local_index, present):
    result = nodal_cube
    extended_count = neighbour_faces.shape[2]
    columns = jnp.arange(extended_count, dtype=jnp.int32)
    for face_id in range(6):
        picker = (local_index[face_id][:, None] == columns[None, :]).astype(jnp.float32)
        across_elements = jnp.einsum(
            "em,cmq->ceq", picker, neighbour_faces[:, face_id ^ 1], precision=lax.Precision.HIGHEST
        )
        change = jnp.where(
            present[face_id][None, :, None], 0.5 * (across_elements - own_faces[:, face_id]), 0.0
        )
        result = result.at[face_slicer(face_id)].add(
            change.reshape(result.shape[0], result.shape[1], 8, 8)
        )
    return result


def bucket_slots(owners, peer_count):
    points = owners.shape[0]
    step_size = math.gcd(points, 2048)
    sub_blocks = step_size // 128
    row_ids = lax.broadcasted_iota(jnp.int32, (128, 128), 0)
    col_ids = lax.broadcasted_iota(jnp.int32, (128, 128), 1)
    lower_triangle = (col_ids < row_ids).astype(jnp.bfloat16)
    targets = jnp.arange(peer_count, dtype=jnp.int32)

    def advance(running, step_owners):
        matches = step_owners.reshape(sub_blocks, 128)[:, :, None] == targets
        one_hot_mask = matches.astype(jnp.bfloat16)
        earlier_entries = jnp.einsum(
            "zw,lwn->lzn", lower_triangle, one_hot_mask, preferred_element_type=jnp.float32
        )
        totals = jnp.sum(one_hot_mask, axis=1, dtype=jnp.float32)
        before = jnp.cumsum(totals, axis=0) - totals + running[None, :]
        position = jnp.sum(jnp.where(matches, earlier_entries + before[:, None, :], 0.0), axis=2)
        return (running + jnp.sum(totals, axis=0), position.reshape(step_size).astype(jnp.int32))

    finished, bucket_slot = lax.scan(
        advance,
        jnp.zeros((peer_count,), jnp.float32),
        owners.reshape(points // step_size, step_size),
    )
    return bucket_slot.reshape(points)


def place_points(payload, owners, bucket_slot, peer_count, capacity):
    channels = payload.shape[0]
    points = owners.shape[0]
    block_size = math.gcd(points, 1024)
    block_count = points // block_size
    peer_ids = jnp.arange(peer_count, dtype=jnp.int32)
    slot_ids = jnp.arange(capacity, dtype=jnp.int32)

    def add_block(placed, block_triple):
        values, block_owners, block_slots = block_triple
        peer_hot = (block_owners[:, None] == peer_ids[None, :]).astype(jnp.float32)
        slot_hot = (block_slots[:, None] == slot_ids[None, :]).astype(jnp.float32)
        spread = values[:, :, None] * peer_hot[None]
        return (
            placed + jnp.einsum("cnp,ns->cps", spread, slot_hot, precision=lax.Precision.HIGHEST),
            None,
        )

    blocks = (
        payload.reshape(channels, block_count, block_size).transpose(1, 0, 2),
        owners.reshape(block_count, block_size),
        bucket_slot.reshape(block_count, block_size),
    )
    placed, unused = lax.scan(
        add_block, jnp.zeros((channels, peer_count, capacity), jnp.float32), blocks
    )
    return placed


def pick_answers(answers, owners, bucket_slot):
    channels, peer_count, capacity = answers.shape
    points = owners.shape[0]
    block_size = math.gcd(points, 1024)
    block_count = points // block_size
    peer_ids = jnp.arange(peer_count, dtype=jnp.int32)
    slot_ids = jnp.arange(capacity, dtype=jnp.int32)

    def one_block(block_pair):
        block_owners, block_slots = block_pair
        peer_hot = (block_owners[:, None] == peer_ids[None, :]).astype(jnp.float32)
        slot_hot = (block_slots[:, None] == slot_ids[None, :]).astype(jnp.float32)
        picked = jnp.einsum("cps,ns->cnp", answers, slot_hot, precision=lax.Precision.HIGHEST)
        return jnp.sum(picked * peer_hot[None], axis=2)

    values = lax.map(
        one_block,
        (owners.reshape(block_count, block_size), bucket_slot.reshape(block_count, block_size)),
    )
    return values.transpose(1, 0, 2).reshape(channels, points)


def interp_block(block_pair, nodal_table):
    coords, elem_ids = block_pair
    block_size = coords.shape[1]
    elem_count = nodal_table.shape[1] // 4
    weights = lagrange(coords)
    one_hot_mask = (elem_ids[:, None] == jnp.arange(elem_count, dtype=jnp.int32)[None, :]).astype(
        jnp.float32
    )
    summed = jnp.zeros((block_size, nodal_table.shape[2]), jnp.float32)
    for half_id in range(2):
        scaled = (
            weights[2][:, 4 * half_id : 4 * half_id + 4, None] * one_hot_mask[:, None, :]
        ).reshape(block_size, 4 * elem_count)
        summed = summed + jnp.dot(
            scaled,
            nodal_table[half_id],
            precision=lax.Precision.HIGHEST,
            preferred_element_type=jnp.float32,
        )
    rs_plane = (weights[0][:, :, None] * weights[1][:, None, :]).reshape(block_size, 1, 64)
    values = jnp.sum(summed.reshape(block_size, nodal_table.shape[2] // 64, 64) * rs_plane, axis=2)
    return values.T


def interpolate(coords, elem_ids, nodal_table):
    peer_count = coords.shape[1]
    slots_each = coords.shape[2]
    point_total = peer_count * slots_each
    block_size = math.gcd(point_total, 4096)
    block_count = point_total // block_size
    coord_blocks = coords.reshape(3, block_count, block_size).transpose(1, 0, 2)
    element_blocks = elem_ids.reshape(block_count, block_size)
    values = lax.map(
        lambda block_pair: interp_block(block_pair, nodal_table), (coord_blocks, element_blocks)
    )
    return values.transpose(1, 0, 2).reshape(3, peer_count, slots_each)


def local(velocity, depart, owner_rank, owner_element_index, neighbours):
    outer_count = lax.axis_size("gx")
    inner_count = lax.axis_size("gy")
    peer_count = outer_count * inner_count
    elem_count = velocity.shape[1]
    points = depart.shape[1]
    capacity = 2 * points // peer_count
    owners = owner_rank[:, 0]
    bucket_slot = bucket_slots(owners, peer_count)
    payload = jnp.concatenate(
        [depart, (owner_element_index + 1).astype(jnp.float32)[None, :]], axis=0
    )
    placed = place_points(payload, owners, bucket_slot, peer_count, capacity)
    send_coords = placed[0:3]
    send_elems = (placed[3:4] - 1.0).astype(jnp.int32)
    nodal_table = (
        velocity.reshape(3, elem_count, 8, 8, 8)
        .transpose(4, 1, 0, 2, 3)
        .reshape(2, 4 * elem_count, 192)
    )
    answers = interpolate(
        lax.all_to_all(send_coords, ("gx", "gy"), split_axis=1, concat_axis=1, tiled=True),
        lax.all_to_all(send_elems, ("gx", "gy"), split_axis=1, concat_axis=1, tiled=True)[0],
        nodal_table,
    )
    answers = lax.all_to_all(answers, ("gx", "gy"), split_axis=1, concat_axis=1, tiled=True)
    departed = pick_answers(answers, owners, bucket_slot)
    nodal_cube = departed.reshape(3, elem_count, 8, 8, 8)
    own_faces = faces_of(nodal_cube)
    extended = with_halo(own_faces, ((("gx", "gy"), 2),), elem_count)
    device_id = lax.axis_index("gx") * inner_count + lax.axis_index("gy")
    first_elem = (device_id - 1) * elem_count
    present = neighbours >= 0
    local_index = jnp.where(present, neighbours - first_elem, 0)
    result = apply_faces_hot(nodal_cube, own_faces, extended, local_index, present)
    return result.reshape(3, elem_count, 512)


def solution(mesh):
    placed = (
        P(None, ("gx", "gy"), None),
        P(None, ("gx", "gy")),
        P(("gx", "gy"), None),
        P(("gx", "gy")),
        P(None, ("gx", "gy")),
    )
    return jax.shard_map(
        local, mesh=mesh, in_specs=placed, out_specs=P(None, ("gx", "gy"), None), check_vma=False
    )
```

profile of v0, /device:TPU:0, one launch (start us, length us, event | category | flops | bytes accessed | tf_op | source)
XLA Modules:
  0.0 390.5 jit_solution(15041983891645134162)
XLA Ops:
  2.2 5.9 %while.55 = (s32[]{:T(128)}, f32[32]{0:T(128)S(1)}, s32[8,2048]{1,0:T(8,128)S(1)}, s32[8,2048]{1,0:T(8,128)S(1)}, s32[]{:T(128)}, /*index=5*/s32[]{:T(128)}, f32[]{:T(128)}) while((s32[]{:T(128)}, f32[32]{0:T(128)S(1)}, s32[8,2048]{1,0:T(8,128)S(1)}, s32[8,2048]{1,0:T(8,128)S(1)}, s32[]{:T(128)}, /*index=5*/s32[]{:T(128)}, ...), condition=%wide.region_5.6_spmd.clone, body=%wide.region_0.5_spmd.clone.sunk | while | flops 17473572 | bytes 88939 | solution.py:109
  8.4 30.2 %while.56 = (s32[]{:T(128)}, f32[4,32,1024]{2,1,0:T(8,128)S(1)}, f32[16,4,1024]{2,1,0:T(4,128)S(1)}, s32[16,1024]{1,0:T(8,128)S(1)}, s32[16,1024]{1,0:T(8,128)S(1)}, /*index=5*/s32[]{:T(128)}, s32[]{:T(128)}) while((s32[]{:T(128)}, f32[4,32,1024]{2,1,0:T(8,128)S(1)}, f32[16,4,1024]{2,1,0:T(4,128)S(1)}, s32[16,1024]{1,0:T(8,128)S(1)}, ...), condition=%wide.region_7.8_spmd.clone, body=%wide.region_6.7_spmd.clone.sunk | while | flops 1612120064 | bytes 1384551 | solution.py:140
  39.4 7.3 %all-to-all-start.1 = ((s32[1,32,1024]{2,0,1:T(1,128)}), s32[1,32,1024]{2,0,1:T(1,128)S(1)}, u32[]{:S(2)}, u32[]{:S(2)}) async-start(s32[1,32,1024]{2,0,1:T(1,128)} %copy.152), calls=%async_computation.1 | async-start | bytes 262144 | tf_op jit(solution)/shard_map/all_to_all | solution.py:228
  47.9 6.7 %all-to-all-done.1 = s32[1,32,1024]{2,0,1:T(1,128)S(1)} async-done(((s32[1,32,1024]{2,0,1:T(1,128)}), s32[1,32,1024]{2,0,1:T(1,128)S(1)}, u32[]{:S(2)}, u32[]{:S(2)}) %all-to-all-start.1) | async-done | bytes 131104 | tf_op jit(solution)/shard_map/all_to_all | solution.py:228
  54.5 2.8 all-to-all-start
  58.4 14.9 %all-to-all-done = f32[3,32,1024]{2,0,1:T(4,128)S(1)} async-done(((f32[3,32,1024]{2,0,1:T(4,128)}), f32[3,32,1024]{2,0,1:T(4,128)S(1)}, u32[]{:S(2)}, u32[]{:S(2)}) %all-to-all-start) | async-done | bytes 393248 | tf_op jit(solution)/shard_map/all_to_all | solution.py:227
  73.8 75.3 %while.53 = (s32[]{:T(128)}, f32[8,3,4096]{2,1,0:T(4,128)}, f32[8,3,4096]{2,0,1:T(8,128)S(1)}, s32[8,4096]{1,0:T(8,128)S(1)}, f32[2,128,192]{2,1,0:T(8,128)S(1)}, /*index=5*/s32[]{:T(128)}) while((s32[]{:T(128)}, f32[8,3,4096]{2,1,0:T(4,128)}, f32[8,3,4096]{2,0,1:T(8,128)S(1)}, s32[8,4096]{1,0:T(8,128)S(1)}, f32[2,128,192]{2,1,0:T(8,128)S(1)}, ...), condition=%wide.region_10.11_spmd, body=%wide.region_8.10_spmd.sunk | while | flops 2421215232 | bytes 27263064 | solution.py:200
  79.3 2.8 convolution_add_fusion.3
  117.0 2.8 convolution_add_fusion.3
  149.1 2.8 all-to-all-start.2
  152.6 15.4 %all-to-all-done.2 = f32[3,32,1024]{2,0,1:T(4,128)S(1)} async-done(((f32[3,32,1024]{2,0,1:T(4,128)}), f32[3,32,1024]{2,0,1:T(4,128)S(1)}, u32[]{:S(2)}, u32[]{:S(2)}) %all-to-all-start.2) | async-done | bytes 393248 | tf_op jit(solution)/shard_map/all_to_all | solution.py:231
  168.2 38.9 %while.54 = (s32[]{:T(128)}, f32[16,3,1024]{2,1,0:T(4,128)S(1)}, s32[16,1024]{1,0:T(8,128)S(1)}, f32[3,32,1024]{2,1,0:T(8,128)S(1)}, s32[16,1024]{1,0:T(8,128)S(1)}, /*index=5*/s32[]{:T(128)}) while((s32[]{:T(128)}, f32[16,3,1024]{2,1,0:T(4,128)S(1)}, s32[16,1024]{1,0:T(8,128)S(1)}, f32[3,32,1024]{2,1,0:T(8,128)S(1)}, ...), condition=%wide.region_13.14_spmd.clone, body=%wide.region_11.13_spmd.clone.sunk | while | flops 1209267200 | bytes 725077 | solution.py:161
  211.1 3.7 fusion.87
  222.7 3.0 copy.161
  225.7 3.0 copy.162
  237.0 5.3 %collective-permute-start = (f32[3,6,32,64]{3,2,1,0:T(8,128)}, f32[3,6,32,64]{3,2,1,0:T(8,128)}, u32[]{:S(2)}, u32[]{:S(2)}) collective-permute-start(f32[3,6,32,64]{3,2,1,0:T(8,128)} %copy.163), channel_id=1, source_target_pairs={{0,1},{1,2},{2,3},{3,4},{4,5},{5,6},{6,7},{7,8},{8,9},{9,10},{10,1... | collective-permute-start | bytes 442376 | tf_op jit(solution)/shard_map/ppermute | solution.py:31
  269.8 8.2 %scatter-add.24 = f32[3,32,8,8,8]{4,3,2,1,0:T(8,128)S(1)} dynamic-update-slice(f32[3,32,8,8,8]{4,3,2,1,0:T(8,128)S(1)} %fusion.66, f32[3,32,8,1,8]{4,3,2,1,0:T(1,128)S(1)} %slice_add_fusion.3, s32[]{:T(128)} %constant.517.clone.1, s32[]{:T(128)} %constant.517.clone.1, s32[]{:T(128)} %constant.517.clone.1, s32[]{:T(128)} %constant.517.clone.1, s32[]{:T(128)} %constant.517.clone.1) | dynamic-update-slice | bytes 49156 | tf_op jit(solution)/shard_map/scatter-add | solution.py:83
  284.4 4.4 %copy.186 = f32[3,32,8,8,1]{4,3,2,1,0:T(8,128)} copy(f32[3,32,8,8,1]{1,3,2,0,4:T(8,128)} %bitcast.294) | data formatting | bytes 49152 | tf_op jit(solution)/shard_map/reshape.208
  290.1 9.1 %scatter-add.25 = f32[3,32,8,8,8]{4,3,2,1,0:T(8,128)S(1)} dynamic-update-slice(f32[3,32,8,8,8]{4,3,2,1,0:T(8,128)S(1)} %scatter-add.24, f32[3,32,8,1,8]{4,3,2,1,0:T(1,128)} %slice_add_fusion.2, s32[]{:T(128)} %constant.517.clone.1, s32[]{:T(128)} %constant.517.clone.1, s32[]{:T(128)} %constant.517.clone.1, s32[]{:T(128)} %constant.527.clone.1, s32[]{:T(128)} %constant.517.clone.1) | dynamic-update-slice | bytes 49156 | tf_op jit(solution)/shard_map/scatter-add | solution.py:83
  299.2 4.2 %slice_add_fusion.1 = f32[3,32,8,8,1]{4,3,2,1,0:T(8,128)} fusion(f32[3,32,8,8,1]{4,3,2,1,0:T(8,128)} %copy.186, f32[3,32,8,8,8]{4,3,2,1,0:T(8,128)S(1)} %scatter-add.25), kind=kLoop, calls=%fused_computation.80 | loop fusion | flops 6144 | bytes 73728 | tf_op jit(solution)/shard_map/add | solution.py:83
  303.4 10.8 %scatter-add.26 = f32[3,32,8,8,8]{4,3,2,1,0:T(8,128)S(1)} dynamic-update-slice(f32[3,32,8,8,8]{4,3,2,1,0:T(8,128)S(1)} %scatter-add.25, f32[3,32,8,8,1]{4,3,2,1,0:T(8,128)} %slice_add_fusion.1, s32[]{:T(128)} %constant.517.clone.1, s32[]{:T(128)} %constant.517.clone.1, s32[]{:T(128)} %constant.517.clone.1, s32[]{:T(128)} %constant.517.clone.1, s32[]{:T(128)} %constant.517.clone.1) | dynamic-update-slice | bytes 49156 | tf_op jit(solution)/shard_map/scatter-add | solution.py:83
  315.5 3.6 copy.190
  319.1 4.4 %slice_add_fusion = f32[3,32,8,8,1]{4,3,2,1,0:T(8,128)} fusion(f32[3,32,8,8,1]{4,3,2,1,0:T(8,128)} %copy.190, f32[3,32,8,8,8]{4,3,2,1,0:T(8,128)S(1)} %scatter-add.26), kind=kLoop, calls=%fused_computation.79 | loop fusion | flops 6144 | bytes 73728 | tf_op jit(solution)/shard_map/add | solution.py:83
  323.5 62.6 %scatter-add.29 = f32[3,32,8,8,8]{4,3,2,1,0:T(8,128)S(1)} dynamic-update-slice(f32[3,32,8,8,8]{4,3,2,1,0:T(8,128)S(1)} %scatter-add.26, f32[3,32,8,8,1]{4,3,2,1,0:T(8,128)} %slice_add_fusion, s32[]{:T(128)} %constant.517.clone.1, s32[]{:T(128)} %constant.517.clone.1, s32[]{:T(128)} %constant.517.clone.1, s32[]{:T(128)} %constant.517.clone.1, s32[]{:T(128)} %constant.527.clone.1) | dynamic-update-slice | bytes 49156 | tf_op jit(solution)/shard_map/scatter-add | solution.py:83
  (388 shorter events, 209.7 us)
Async XLA Ops:
  0.0 8.2 %copy-start.4 = (s32[16384,1]{0,1:T(1,128)S(1)}, s32[16384,1]{0,1:T(1,128)}, u32[]{:S(2)}) copy-start(s32[16384,1]{0,1:T(1,128)} %param.27) | copy-start | bytes 196612
  0.0 8.1 %copy-start.8 = (s32[16384]{0:T(1024)S(1)}, s32[16384]{0:T(1024)}, u32[]{:S(2)}) copy-start(s32[16384]{0:T(1024)} %param.28) | copy-start | bytes 196612
  0.0 8.2 %copy-start.3 = (f32[3,16384]{1,0:T(4,128)S(1)}, f32[3,16384]{1,0:T(4,128)}, u32[]{:S(2)}) copy-start(f32[3,16384]{1,0:T(4,128)} %param.26) | copy-start | bytes 589828
  8.3 49.0 %copy-start.7 = (f32[3,32,512]{2,1,0:T(8,128)S(1)}, f32[3,32,512]{2,1,0:T(8,128)}, u32[]{:S(2)}) copy-start(f32[3,32,512]{2,1,0:T(8,128)} %param.25) | copy-start | bytes 589828
  39.4 15.2 %all-to-all-start.1 = ((s32[1,32,1024]{2,0,1:T(1,128)}), s32[1,32,1024]{2,0,1:T(1,128)S(1)}, u32[]{:S(2)}, u32[]{:S(2)}) async-start(s32[1,32,1024]{2,0,1:T(1,128)} %copy.152), calls=%async_computation.1 | async-start | bytes 262144 | tf_op jit(solution)/shard_map/all_to_all | solution.py:228
  54.5 18.8 %all-to-all-start = ((f32[3,32,1024]{2,0,1:T(4,128)}), f32[3,32,1024]{2,0,1:T(4,128)S(1)}, u32[]{:S(2)}, u32[]{:S(2)}) async-start(f32[3,32,1024]{2,0,1:T(4,128)} %bitcast.225), calls=%async_computation | async-start | bytes 1048576 | tf_op jit(solution)/shard_map/all_to_all | solution.py:227
  73.8 78.2 %copy-start.9 = (s32[6,32]{1,0:T(8,128)S(1)}, s32[6,32]{1,0:T(8,128)}, u32[]{:S(2)}) copy-start(s32[6,32]{1,0:T(8,128)} %param.29) | copy-start | bytes 2308
  149.1 18.8 %all-to-all-start.2 = ((f32[3,32,1024]{2,0,1:T(4,128)}), f32[3,32,1024]{2,0,1:T(4,128)S(1)}, u32[]{:S(2)}, u32[]{:S(2)}) async-start(f32[3,32,1024]{2,0,1:T(4,128)} %bitcast.27), calls=%async_computation.2 | async-start | bytes 1048576 | tf_op jit(solution)/shard_map/all_to_all | solution.py:231
  222.7 6.0 %copy-start.2 = (f32[3,32,1,8,8]{1,4,3,0,2:T(8,128)S(1)}, f32[3,32,1,8,8]{1,4,3,0,2:T(8,128)}, u32[]{:S(2)}) copy-start(f32[3,32,1,8,8]{1,4,3,0,2:T(8,128)} %copy.158) | copy-start | bytes 73732
  225.7 17.2 %copy-start.1 = (f32[3,32,1,8,8]{1,4,3,0,2:T(8,128)S(1)}, f32[3,32,1,8,8]{1,4,3,0,2:T(8,128)}, u32[]{:S(2)}) copy-start(f32[3,32,1,8,8]{1,4,3,0,2:T(8,128)} %copy.157) | copy-start | bytes 73732
  235.7 13.2 %collective-permute-start.1 = (f32[3,6,32,64]{3,2,1,0:T(8,128)}, f32[3,6,32,64]{3,2,1,0:T(8,128)}, u32[]{:S(2)}, u32[]{:S(2)}) collective-permute-start(f32[3,6,32,64]{3,2,1,0:T(8,128)} %copy.163), channel_id=1, source_target_pairs={{1,0},{2,1},{3,2},{4,3},{5,4},{6,5},{7,6},{8,7},{9,8},{10,9},{11,1... | collective-permute-start | bytes 442376 | tf_op jit(solution)/shard_map/ppermute | solution.py:33
  237.0 15.6 %collective-permute-start = (f32[3,6,32,64]{3,2,1,0:T(8,128)}, f32[3,6,32,64]{3,2,1,0:T(8,128)}, u32[]{:S(2)}, u32[]{:S(2)}) collective-permute-start(f32[3,6,32,64]{3,2,1,0:T(8,128)} %copy.163), channel_id=1, source_target_pairs={{0,1},{1,2},{2,3},{3,4},{4,5},{5,6},{6,7},{7,8},{8,9},{9,10},{10,1... | collective-permute-start | bytes 442376 | tf_op jit(solution)/shard_map/ppermute | solution.py:31
  243.6 13.6 %copy-start.6 = (f32[3,32,64]{2,1,0:T(8,128)S(1)}, f32[3,32,64]{2,1,0:T(8,128)}, u32[]{:S(2)}) copy-start(f32[3,32,64]{2,1,0:T(8,128)} %copy.168) | copy-start | bytes 73732
  243.6 13.6 %copy-start.12 = (pred[32]{0:T(512)(128)(4,1)S(1)}, pred[32]{0:T(512)(128)(4,1)}, u32[]{:S(2)}) copy-start(pred[32]{0:T(512)(128)(4,1)} %get-tuple-element.426) | copy-start | bytes 100
  251.0 12.2 %copy-start.10 = (s32[32]{0:T(128)S(1)}, s32[32]{0:T(128)}, u32[]{:S(2)}) copy-start(s32[32]{0:T(128)} %get-tuple-element.418) | copy-start | bytes 388
  256.4 0.8 copy-start
  303.4 10.8 %copy-start.5 = (f32[3,32,64]{2,1,0:T(8,128)S(1)}, f32[3,32,64]{2,1,0:T(8,128)}, u32[]{:S(2)}) copy-start(f32[3,32,64]{2,1,0:T(8,128)} %copy.188) | copy-start | bytes 73732
  303.4 10.8 %copy-start.11 = (pred[32]{0:T(512)(128)(4,1)S(1)}, pred[32]{0:T(512)(128)(4,1)}, u32[]{:S(2)}) copy-start(pred[32]{0:T(512)(128)(4,1)} %get-tuple-element.421) | copy-start | bytes 100
where the time goes:
time: 393 us; the launch traced here: 391 us
  local copies, waits for them, and re-layouts  172 us (44%)
  matrix products  120 us (31%)
  waiting for transfers between devices  38.6 us (10%)
  other arithmetic  37.5 us (10%)
  starting transfers between devices  19.5 us (5%)
    scatter-add x5, local copies, waits for them, and re-layouts, apply_faces_hot(): result.at[face_slicer(face_id)]  93 us
    dot_general x16, matrix products, interp_block(): jnp.dot(scaled, nodal_table[half_id], precision=lax.Precision.HIGHEST, pr...  44 us
    dot_general x16, matrix products, one_block(): jnp.einsum('cps,ns->cnp', answers, slot_hot, precision=lax.Precision.HIGH...  37.5 us
    dot_general x16, matrix products, add_block(): jnp.einsum('cnp,ns->cps', spread, slot_hot, precision=lax.Precision.HIGHEST)  28.8 us
    slice x8, local copies, waits for them, and re-layouts, faces_of(): nodal_cube[face_slicer(face_id)].reshape(shape_lead)  16.5 us
    all_to_all x1, waiting for transfers between devices, local(): lax.all_to_all(answers, ('gx', 'gy'), split_axis=1, concat_axis=1, tiled=...  15.4 us
    all_to_all x1, waiting for transfers between devices, local(): lax.all_to_all(send_coords, ('gx', 'gy'), split_axis=1, concat_axis=1, ti...  14.9 us
    another operation x7, local copies, waits for them, and re-layouts  14.9 us
  transfers between devices with their start and end apart: 5, of which 4 were waited for; matrix products, arithmetic and copies ran while one was open for 3% of the time, Pallas kernels for 0%

commit v1 on v0

v1 whole, which is shorter than its diff:
```python
import functools
import math

import jax
import jax.numpy as jnp
import numpy as np
from jax import lax
from jax.experimental import pallas as pl
from jax.experimental.pallas import tpu as pltpu
from jax.sharding import PartitionSpec as P

GLL_POINTS = np.array(
    [
        -1.0,
        -0.8717401485096066,
        -0.5917001814331423,
        -0.2092992179024789,
        0.2092992179024789,
        0.5917001814331423,
        0.8717401485096066,
        1.0,
    ]
)
F32, BF16 = jnp.float32, jnp.bfloat16


def lagrange_constants():
    table = np.zeros((8, 128))
    for i in range(8):
        table[i, 0] = 1.0 / np.prod([GLL_POINTS[i] - GLL_POINTS[m] for m in range(8) if m != i])
        for r in range(1, 8):
            table[i, r] = GLL_POINTS[(i + r) % 8]
    return table.astype(np.float32)


def face_selector():
    cube = np.arange(512).reshape(8, 8, 8)
    faces = [cube[0], cube[7], cube[:, 0], cube[:, 7], cube[:, :, 0], cube[:, :, 7]]
    nodes = np.concatenate([face.reshape(-1) for face in faces])
    return (np.arange(512)[:, None] == nodes[None, :]).astype(np.float32)


def split2(x):
    hi = x.astype(BF16).astype(F32)
    return hi, x - hi


def dot(a, b):
    return lax.dot_general(a, b, (((1,), (0,)), ((), ())), preferred_element_type=F32)


def dot_nt(a, b):
    return lax.dot_general(a, b, (((1,), (1,)), ((), ())), preferred_element_type=F32)


def place_kernel(peers, capacity, sub, owner_ref, coords_ref, elem_ref, upper_ref, send_ref, slot_ref, acc, carry):
    step = pl.program_id(0)

    @pl.when(step == 0)
    def _():
        acc[...] = jnp.zeros_like(acc)
        carry[...] = jnp.zeros_like(carry)

    block = owner_ref.shape[1]
    upper = upper_ref[...]
    peer_rows = lax.broadcasted_iota(jnp.int32, (peers, sub), 0)
    slots = []
    running = carry[:, 0:1]
    for part in range(block // sub):
        owner = owner_ref[:, part * sub : (part + 1) * sub]
        match = peer_rows == owner
        hot = match.astype(F32)
        earlier = dot(hot.astype(BF16), upper) + running
        slots.append(jnp.sum(jnp.where(match, earlier, 0.0), axis=0, keepdims=True))
        running = running + jnp.sum(hot, axis=1, keepdims=True)
    carry[...] = jnp.broadcast_to(running, carry.shape)
    slot = jnp.concatenate(slots, axis=1).astype(jnp.int32)
    slot_ref[...] = slot
    owner = jnp.broadcast_to(owner_ref[...], (8, block))
    hi, lo = split2(coords_ref[...])
    values = jnp.concatenate([hi, elem_ref[...].astype(F32), lo, jnp.zeros((1, block), F32)], axis=0)
    spread = jnp.concatenate([jnp.where(owner == p, values, 0.0) for p in range(peers)], axis=0).astype(BF16)
    for at in range(0, capacity, 256):
        width = min(256, capacity - at)
        rows = lax.broadcasted_iota(jnp.int32, (width, block), 0) + at
        hot = (rows == slot).astype(F32).astype(BF16)
        acc[:, at : at + width] += dot_nt(spread, hot)

    @pl.when(step == pl.num_programs(0) - 1)
    def _():
        for p in range(peers):
            both = acc[8 * p : 8 * p + 8]
            send_ref[p] = jnp.concatenate([both[0:3] + both[4:7], both[3:4]], axis=0)


def place(owner, coords, elem, peers, capacity):
    points = owner.shape[1]
    block, sub = math.gcd(points, 1024), math.gcd(points, 256)
    upper = np.triu(np.ones((sub, sub), np.float32), 1)
    return pl.pallas_call(
        functools.partial(place_kernel, peers, capacity, sub),
        grid=(points // block,),
        in_specs=[
            pl.BlockSpec((1, block), lambda i: (0, i)),
            pl.BlockSpec((3, block), lambda i: (0, i)),
            pl.BlockSpec((1, block), lambda i: (0, i)),
            pl.BlockSpec((sub, sub), lambda i: (0, 0)),
        ],
        out_specs=[
            pl.BlockSpec((peers, 4, capacity), lambda i: (0, 0, 0)),
            pl.BlockSpec((1, block), lambda i: (0, i)),
        ],
        out_shape=[
            jax.ShapeDtypeStruct((peers, 4, capacity), F32),
            jax.ShapeDtypeStruct((1, points), jnp.int32),
        ],
        scratch_shapes=[pltpu.VMEM((8 * peers, capacity), F32), pltpu.VMEM((peers, 128), F32)],
        compiler_params=pltpu.CompilerParams(dimension_semantics=("arbitrary",)),
        name="place",
    )(owner, coords, elem, jnp.asarray(upper, BF16))


def interp_kernel(elems, chunk, points_ref, table_ref, const_ref, out_ref, stacked):
    @pl.when(pl.program_id(0) == 0)
    def _():
        hi, lo = split2(table_ref[...])
        stacked[...] = jnp.concatenate([hi, hi, lo], axis=1).astype(BF16)

    slots = points_ref.shape[2]
    for at in range(0, slots, chunk):
        x = points_ref[0, :, at : at + chunk]
        weights = []
        for d in range(3):
            coord = jnp.broadcast_to(x[d : d + 1], (8, chunk))
            w = const_ref[:, 0:1] * (coord - const_ref[:, 1:2])
            for r in range(2, 8):
                w = w * (coord - const_ref[:, r : r + 1])
            weights.append(w)
        elem = jnp.broadcast_to(x[3:4], (8, chunk))
        hi, lo = split2(weights[2])
        picks = [elem == float(e) for e in range(elems)]
        a_hi = jnp.concatenate([jnp.where(pick, hi, 0.0) for pick in picks], axis=0).astype(BF16)
        a_lo = jnp.concatenate([jnp.where(pick, lo, 0.0) for pick in picks], axis=0).astype(BF16)
        summed = dot(stacked[...], jnp.concatenate([a_hi, a_lo, a_hi], axis=0))
        results = []
        for c in range(3):
            total = None
            for i in range(8):
                term = summed[64 * c + 8 * i : 64 * c + 8 * i + 8] * weights[0][i : i + 1]
                total = term if total is None else total + term
            results.append(jnp.sum(total * weights[1], axis=0, keepdims=True))
        out_ref[0, :, at : at + chunk] = jnp.concatenate(results, axis=0)


def interpolate(points, table):
    peers, _, slots = points.shape
    elems = table.shape[1] // 8
    chunk = math.gcd(slots, 256)
    return pl.pallas_call(
        functools.partial(interp_kernel, elems, chunk),
        grid=(peers,),
        in_specs=[
            pl.BlockSpec((1, 4, slots), lambda i: (i, 0, 0)),
            pl.BlockSpec(table.shape, lambda i: (0, 0)),
            pl.BlockSpec((8, 128), lambda i: (0, 0)),
        ],
        out_specs=pl.BlockSpec((1, 3, slots), lambda i: (i, 0, 0)),
        out_shape=jax.ShapeDtypeStruct((peers, 3, slots), F32),
        scratch_shapes=[pltpu.VMEM((192, 3 * table.shape[1]), BF16)],
        compiler_params=pltpu.CompilerParams(dimension_semantics=("arbitrary",)),
        name="interp",
    )(points, table, jnp.asarray(lagrange_constants()))


def pick_kernel(peers, per_step, answers_ref, owner_ref, slot_ref, select_ref, out_ref, faces_ref, halves):
    step = pl.program_id(0)
    capacity = answers_ref.shape[2]

    @pl.when(step == 0)
    def _():
        gap = jnp.zeros((1, capacity), F32)
        for p in range(0, peers, 2):
            rows = []
            for q in (p, p + 1):
                hi, lo = split2(answers_ref[q])
                rows += [hi, gap, lo, gap]
            halves[8 * p : 8 * p + 16] = jnp.concatenate(rows, axis=0).astype(BF16)

    for at in range(per_step):
        nodes = slice(512 * at, 512 * at + 512)
        slot = slot_ref[:, nodes]
        rows = lax.broadcasted_iota(jnp.int32, (capacity, 512), 0)
        hot = (rows == slot).astype(F32).astype(BF16)
        picked = dot(halves[...], hot)
        owner = jnp.broadcast_to(owner_ref[:, nodes], (8, 512))
        total = jnp.zeros((8, 512), F32)
        for p in range(peers):
            total = total + jnp.where(owner == p, picked[8 * p : 8 * p + 8], 0.0)
        for c in range(3):
            out_ref[c, pl.ds(step * per_step + at, 1), :] = total[c : c + 1] + total[c + 4 : c + 5]

    @pl.when(step == pl.num_programs(0) - 1)
    def _():
        for c in range(3):
            hi, lo = split2(out_ref[c])
            mid, low = split2(lo)
            sel = select_ref[...]
            faces_ref[c] = dot(hi.astype(BF16), sel) + dot(mid.astype(BF16), sel) + dot(low.astype(BF16), sel)


def pick(answers, owner, slot, elems, select):
    peers, _, capacity = answers.shape
    points = owner.shape[1]
    per_step = math.gcd(elems, 2)
    block = per_step * 512
    return pl.pallas_call(
        functools.partial(pick_kernel, peers, per_step),
        grid=(points // block,),
        in_specs=[
            pl.BlockSpec(answers.shape, lambda i: (0, 0, 0)),
            pl.BlockSpec((1, block), lambda i: (0, i)),
            pl.BlockSpec((1, block), lambda i: (0, i)),
            pl.BlockSpec((512, 384), lambda i: (0, 0)),
        ],
        out_specs=[
            pl.BlockSpec((3, elems, 512), lambda i: (0, 0, 0)),
            pl.BlockSpec((3, elems, 384), lambda i: (0, 0, 0)),
        ],
        out_shape=[
            jax.ShapeDtypeStruct((3, elems, 512), F32),
            jax.ShapeDtypeStruct((3, elems, 384), F32),
        ],
        scratch_shapes=[pltpu.VMEM((8 * peers, capacity), BF16)],
        compiler_params=pltpu.CompilerParams(dimension_semantics=("arbitrary",)),
        name="pick",
    )(answers, owner, slot, select)


def faces_kernel(interp_ref, own_ref, prev_ref, next_ref, index_ref, select_ref, out_ref):
    elems = interp_ref.shape[1]
    index = index_ref[...]
    columns = lax.broadcasted_iota(jnp.int32, (6 * elems, 3 * elems), 1)
    picker = (columns == index).astype(F32).astype(BF16)
    present = (index >= 0).astype(F32)
    for c in range(3):
        own = own_ref[c]
        extended = jnp.concatenate([prev_ref[c], own, next_ref[c]], axis=0)
        hi, lo = split2(extended)
        across = dot(picker, hi.astype(BF16)) + dot(picker, lo.astype(BF16))
        changes = []
        for f in range(6):
            g = f ^ 1
            rows = slice(f * elems, (f + 1) * elems)
            other = across[rows, 64 * g : 64 * g + 64]
            changes.append(0.5 * (other - present[rows] * own[:, 64 * f : 64 * f + 64]))
        hi, lo = split2(jnp.concatenate(changes, axis=1))
        sel = select_ref[...]
        out_ref[c] = interp_ref[c] + dot_nt(hi.astype(BF16), sel) + dot_nt(lo.astype(BF16), sel)


def local(velocity, depart, owner_rank, owner_element_index, neighbours):
    axes = ("gx", "gy")
    inner_count = lax.axis_size("gy")
    peers = lax.axis_size("gx") * inner_count
    elems = velocity.shape[1]
    points = depart.shape[1]
    capacity = 2 * points // peers
    owner = owner_rank.reshape(1, points)
    select = jnp.asarray(face_selector(), BF16)
    send, slot = place(owner, depart, owner_element_index.reshape(1, points), peers, capacity)
    received = lax.all_to_all(send, axes, split_axis=0, concat_axis=0, tiled=True)
    table = velocity.reshape(3, elems, 64, 8).transpose(0, 2, 1, 3).reshape(192, elems * 8)
    answers = interpolate(received, table)
    answers = lax.all_to_all(answers, axes, split_axis=0, concat_axis=0, tiled=True)
    interp, faces = pick(answers, owner, slot, elems, select)
    before = lax.ppermute(faces, axes, [(i, i + 1) for i in range(peers - 1)])
    after = lax.ppermute(faces, axes, [(i + 1, i) for i in range(peers - 1)])
    device_id = lax.axis_index("gx") * inner_count + lax.axis_index("gy")
    index = jnp.where(neighbours >= 0, neighbours - (device_id - 1) * elems, -1)
    return pl.pallas_call(
        faces_kernel,
        out_shape=jax.ShapeDtypeStruct((3, elems, 512), F32),
        name="faces",
    )(interp, faces, before, after, index.reshape(6 * elems, 1), select)


def solution(mesh):
    placed = (
        P(None, ("gx", "gy"), None),
        P(None, ("gx", "gy")),
        P(("gx", "gy"), None),
        P(("gx", "gy")),
        P(None, ("gx", "gy")),
    )
    return jax.shard_map(
        local, mesh=mesh, in_specs=placed, out_specs=P(None, ("gx", "gy"), None), check_vma=False
    )
```

time: 393 us -> 119 us (0.30)
  local copies, waits for them, and re-layouts: 172 us -> 5.05 us
  matrix products: 120 us -> 0 us
  Pallas kernels: 0 us -> 59.6 us
  other arithmetic: 37.5 us -> 0.01 us
  starting transfers between devices: 19.5 us -> 14.1 us
    dot_general x62 -> x0, matrix products: 120 us -> none  [the longest x16 44 us: interp_block(): jnp.dot(scaled, nodal_table[half_id], precision=lax.Precision.HIGHEST, pr...]
    scatter-add x5 -> x0, local copies, waits for them, and re-layouts: 93 us -> none  [apply_faces_hot(): result.at[face_slicer(face_id)]]
    pallas_call x0 -> x4, Pallas kernels: none -> 59.6 us  [the longest x1 22.5 us: interpolate(): pl.pallas_call(functools.partial(interp_kernel, elems, chunk), grid=(peer...]
    another operation x28 -> x0, local copies, waits for them, and re-layouts: 30.5 us -> none
    slice x16 -> x0, local copies, waits for them, and re-layouts: 16.6 us -> none  [the longest x8 16.5 us: faces_of(): nodal_cube[face_slicer(face_id)].reshape(shape_lead)]
    mul x24 -> x0, other arithmetic: 16.3 us -> none  [the longest x8 11.8 us: lagrange(): factor * ((coords - float(GLL_POINTS[other])) / float(GLL_POINTS[node_id]...]
    add x20 -> x0, other arithmetic: 11.4 us -> none  [the longest x4 11.3 us: apply_faces_hot(): result.at[face_slicer(face_id)]]
    dynamic_update_slice x32 -> x0, local copies, waits for them, and re-layouts: 7.01 us -> none  [the longest x8 5.14 us: interpolate(): lax.map(lambda block_pair: interp_block(block_pair, nodal_table), (coord_...]
  transfers between devices with their start and end apart: 5 -> 4, of which waited for: 4 -> 4; matrix products, arithmetic and copies ran while one was open for 3% -> 2% of each run, Pallas kernels for 0% -> 0%
where the time goes in v1:
time: 119 us; the launch traced here: 116 us
  Pallas kernels  59.6 us (50%)
  waiting for transfers between devices  37.6 us (32%)
  starting transfers between devices  14.1 us (12%)
  local copies, waits for them, and re-layouts  5.05 us (4%)
    pallas_call x1, Pallas kernels, interpolate(): pl.pallas_call(functools.partial(interp_kernel, elems, chunk), grid=(peer...  22.5 us
    pallas_call x1, Pallas kernels, place(): pl.pallas_call(functools.partial(place_kernel, peers, capacity, sub), gri...  17.6 us
    all_to_all x1, waiting for transfers between devices, local(): lax.all_to_all(answers, axes, split_axis=0, concat_axis=0, tiled=True)  16.2 us
    pallas_call x1, Pallas kernels, pick(): pl.pallas_call(functools.partial(pick_kernel, peers, per_step), grid=(poi...  16 us
    all_to_all x1, waiting for transfers between devices, local(): lax.all_to_all(send, axes, split_axis=0, concat_axis=0, tiled=True)  14.2 us
    all_to_all x1, starting transfers between devices, local(): lax.all_to_all(send, axes, split_axis=0, concat_axis=0, tiled=True)  7.33 us
    ppermute x1, waiting for transfers between devices, local(): after = lax.ppermute(faces, axes, [(i + 1, i) for i in range(peers - 1)])  5.59 us
    pallas_call x1, Pallas kernels, local(): pl.pallas_call(faces_kernel, out_shape=jax.ShapeDtypeStruct((3, elems, 51...  3.56 us
  transfers between devices with their start and end apart: 4, of which 4 were waited for; matrix products, arithmetic and copies ran while one was open for 2% of the time, Pallas kernels for 0%

profile of v1, /device:TPU:0, one launch (start us, length us, event | category | flops | bytes accessed | tf_op | source)
XLA Modules:
  0.0 116.4 jit_solution(14405253005386112534)
XLA Ops:
  0.0 17.6 %place.1 = (f32[32,4,1024]{2,1,0:T(4,128)}, s32[1,16384]{1,0:T(1,128)}) custom-call(s32[1,16384]{1,0:T(1,128)} %bitcast.8, f32[3,16384]{1,0:T(4,128)} %coords_ref.1, s32[1,16384]{1,0:T(1,128)} %bitcast.10, bf16[256,256]{1,0:T(8,128)(2,1)} %constant.25.clone.upper_ref), custom_call_target="tpu_custom_call" | custom-call | tf_op jit(solution)/shard_map/place/pallas_call | solution.py:100
  17.6 0.0 copy-start.2
  17.6 7.3 %all-to-all-start = ((f32[32,4,1024]{2,1,0:T(4,128)}), f32[32,4,1024]{2,1,0:T(4,128)S(1)}, u32[]{:S(2)}, u32[]{:S(2)}) async-start(f32[32,4,1024]{2,1,0:T(4,128)} %get-tuple-element.9), calls=%async_computation | async-start | bytes 1048576 | tf_op jit(solution)/shard_map/all_to_all | solution.py:271
  24.9 0.0 copy-done.2
  24.9 0.3 copy.10
  25.2 0.7 copy.11
  25.9 0.3 reshape.18
  26.2 0.8 copy.12.table_ref
  27.0 14.2 %all-to-all-done.points_ref = f32[32,4,1024]{2,1,0:T(4,128)S(1)} async-done(((f32[32,4,1024]{2,1,0:T(4,128)}), f32[32,4,1024]{2,1,0:T(4,128)S(1)}, u32[]{:S(2)}, u32[]{:S(2)}) %all-to-all-start) | async-done | bytes 524320 | tf_op jit(solution)/shard_map/all_to_all | solution.py:271
  41.1 0.8 copy-done.1
  41.9 22.5 %interp.1 = f32[32,3,1024]{2,1,0:T(4,128)} custom-call(f32[32,4,1024]{2,1,0:T(4,128)} %copy-done.1, f32[192,256]{1,0:T(8,128)} %copy.12.table_ref, f32[8,128]{1,0:T(8,128)} %constant.26.clone.const_ref), custom_call_target="tpu_custom_call" | custom-call | tf_op jit(solution)/shard_map/interp/pallas_call | solution.py:159
  64.4 2.6 %all-to-all-start.1 = ((f32[32,3,1024]{2,1,0:T(4,128)}), f32[32,3,1024]{2,1,0:T(4,128)S(1)}, u32[]{:S(2)}, u32[]{:S(2)}) async-start(f32[32,3,1024]{2,1,0:T(4,128)} %interp.1), calls=%async_computation.1 | async-start | bytes 1048576 | tf_op jit(solution)/shard_map/all_to_all | solution.py:274
  67.0 16.2 %all-to-all-done.1.answers_ref = f32[32,3,1024]{2,1,0:T(4,128)S(1)} async-done(((f32[32,3,1024]{2,1,0:T(4,128)}), f32[32,3,1024]{2,1,0:T(4,128)S(1)}, u32[]{:S(2)}, u32[]{:S(2)}) %all-to-all-start.1) | async-done | bytes 393248 | tf_op jit(solution)/shard_map/all_to_all | solution.py:274
  83.3 0.8 copy-done
  84.1 16.0 %pick.1 = (f32[3,32,512]{2,1,0:T(8,128)}, f32[3,32,384]{2,1,0:T(8,128)}) custom-call(f32[32,3,1024]{2,1,0:T(4,128)} %copy-done, s32[1,16384]{1,0:T(1,128)} %bitcast.9, s32[1,16384]{1,0:T(1,128)} %get-tuple-element.10.slot_ref, bf16[512,384]{1,0:T(8,128)(2,1)} %constant.24.clone.select_ref), custom_call_target="tpu_custom_call" | custom-call | tf_op jit(solution)/shard_map/pick/pallas_call | solution.py:216
  100.1 2.8 %collective-permute-start = (f32[3,32,384]{2,1,0:T(8,128)}, f32[3,32,384]{2,1,0:T(8,128)S(1)}, u32[]{:S(2)}, u32[]{:S(2)}) collective-permute-start(f32[3,32,384]{2,1,0:T(8,128)} %get-tuple-element.12.own_ref), channel_id=1, source_target_pairs={{0,1},{1,2},{2,3},{3,4},{4,5},{5,6},{6,7},{7,8},{8,9},{9,10},{10,1... | collective-permute-start | bytes 442376 | tf_op jit(solution)/shard_map/ppermute | solution.py:276
  102.9 1.3 %collective-permute-start.1 = (f32[3,32,384]{2,1,0:T(8,128)}, f32[3,32,384]{2,1,0:T(8,128)S(1)}, u32[]{:S(2)}, u32[]{:S(2)}) collective-permute-start(f32[3,32,384]{2,1,0:T(8,128)} %get-tuple-element.12.own_ref), channel_id=1, source_target_pairs={{1,0},{2,1},{3,2},{4,3},{5,4},{6,5},{7,6},{8,7},{9,8},{10,9},{11,1... | collective-permute-start | bytes 442376 | tf_op jit(solution)/shard_map/ppermute | solution.py:277
  104.2 0.0 copy-done.5
  104.3 0.8 reshape.20.index_ref
  105.0 1.6 %collective-permute-done.prev_ref = f32[3,32,384]{2,1,0:T(8,128)S(1)} collective-permute-done((f32[3,32,384]{2,1,0:T(8,128)}, f32[3,32,384]{2,1,0:T(8,128)S(1)}, u32[]{:S(2)}, u32[]{:S(2)}) %collective-permute-start) | collective-permute-done | bytes 147488 | tf_op jit(solution)/shard_map/ppermute | solution.py:276
  106.6 5.6 %collective-permute-done.1.next_ref = f32[3,32,384]{2,1,0:T(8,128)S(1)} collective-permute-done((f32[3,32,384]{2,1,0:T(8,128)}, f32[3,32,384]{2,1,0:T(8,128)S(1)}, u32[]{:S(2)}, u32[]{:S(2)}) %collective-permute-start.1) | collective-permute-done | bytes 147488 | tf_op jit(solution)/shard_map/ppermute | solution.py:277
  112.2 0.0 copy-done.3
  112.2 0.7 copy-done.4
  112.9 3.6 %faces.1 = f32[3,32,512]{2,1,0:T(8,128)} custom-call(f32[3,32,512]{2,1,0:T(8,128)} %get-tuple-element.11.interp_ref, f32[3,32,384]{2,1,0:T(8,128)} %get-tuple-element.12.own_ref, f32[3,32,384]{2,1,0:T(8,128)} %copy-done.3, f32[3,32,384]{2,1,0:T(8,128)} %copy-done.4, s32[192,1]{1,0:T(8,128)} %reshape.20.index_ref, bf16[512,384]{1,0:T(8,128)(2,1)} %constant.24.clone.select_ref), custom_call_target="tpu_custom_call" | custom-call | tf_op jit(solution)/shard_map/faces/pallas_call | solution.py:280
  (6 shorter events, 0.0 us)
Async XLA Ops:
  17.6 7.3 %copy-start.2 = (f32[3,32,512]{2,1,0:T(8,128)S(1)}, f32[3,32,512]{2,1,0:T(8,128)}, u32[]{:S(2)}) copy-start(f32[3,32,512]{2,1,0:T(8,128)} %param.8) | copy-start | bytes 589828
  17.6 23.6 %all-to-all-start = ((f32[32,4,1024]{2,1,0:T(4,128)}), f32[32,4,1024]{2,1,0:T(4,128)S(1)}, u32[]{:S(2)}, u32[]{:S(2)}) async-start(f32[32,4,1024]{2,1,0:T(4,128)} %get-tuple-element.9), calls=%async_computation | async-start | bytes 1048576 | tf_op jit(solution)/shard_map/all_to_all | solution.py:271
  41.1 0.8 copy-start.1
  64.4 18.8 %all-to-all-start.1 = ((f32[32,3,1024]{2,1,0:T(4,128)}), f32[32,3,1024]{2,1,0:T(4,128)S(1)}, u32[]{:S(2)}, u32[]{:S(2)}) async-start(f32[32,3,1024]{2,1,0:T(4,128)} %interp.1), calls=%async_computation.1 | async-start | bytes 1048576 | tf_op jit(solution)/shard_map/all_to_all | solution.py:274
  83.3 0.8 copy-start
  84.1 20.2 %copy-start.5 = (s32[6,32]{1,0:T(8,128)S(1)}, s32[6,32]{1,0:T(8,128)}, u32[]{:S(2)}) copy-start(s32[6,32]{1,0:T(8,128)} %param.12) | copy-start | bytes 2308
  100.1 6.5 %collective-permute-start = (f32[3,32,384]{2,1,0:T(8,128)}, f32[3,32,384]{2,1,0:T(8,128)S(1)}, u32[]{:S(2)}, u32[]{:S(2)}) collective-permute-start(f32[3,32,384]{2,1,0:T(8,128)} %get-tuple-element.12.own_ref), channel_id=1, source_target_pairs={{0,1},{1,2},{2,3},{3,4},{4,5},{5,6},{6,7},{7,8},{8,9},{9,10},{10,1... | collective-permute-start | bytes 442376 | tf_op jit(solution)/shard_map/ppermute | solution.py:276
  102.9 9.3 %collective-permute-start.1 = (f32[3,32,384]{2,1,0:T(8,128)}, f32[3,32,384]{2,1,0:T(8,128)S(1)}, u32[]{:S(2)}, u32[]{:S(2)}) collective-permute-start(f32[3,32,384]{2,1,0:T(8,128)} %get-tuple-element.12.own_ref), channel_id=1, source_target_pairs={{1,0},{2,1},{3,2},{4,3},{5,4},{6,5},{7,6},{8,7},{9,8},{10,9},{11,1... | collective-permute-start | bytes 442376 | tf_op jit(solution)/shard_map/ppermute | solution.py:277
  106.6 5.6 %copy-start.3 = (f32[3,32,384]{2,1,0:T(8,128)}, f32[3,32,384]{2,1,0:T(8,128)S(1)}, u32[]{:S(2)}) copy-start(f32[3,32,384]{2,1,0:T(8,128)S(1)} %collective-permute-done.prev_ref) | copy-start | bytes 442372
  112.2 0.7 copy-start.4

commit v2 on v1

--- a/solution.py
+++ b/solution.py
@@ -22,6 +22,7 @@
     ]
 )
 F32, BF16 = jnp.float32, jnp.bfloat16
+MESH = pl.DeviceIdType.MESH
 
 
 def lagrange_constants():
@@ -120,15 +121,9 @@
     )(owner, coords, elem, jnp.asarray(upper, BF16))
 
 
-def interp_kernel(elems, chunk, points_ref, table_ref, const_ref, out_ref, stacked):
-    @pl.when(pl.program_id(0) == 0)
-    def _():
-        hi, lo = split2(table_ref[...])
-        stacked[...] = jnp.concatenate([hi, hi, lo], axis=1).astype(BF16)
-
-    slots = points_ref.shape[2]
+def interp_chunks(elems, chunk, load, store, slots, stacked, const_ref):
     for at in range(0, slots, chunk):
-        x = points_ref[0, :, at : at + chunk]
+        x = load(slice(at, at + chunk))
         weights = []
         for d in range(3):
             coord = jnp.broadcast_to(x[d : d + 1], (8, chunk))
@@ -149,35 +144,150 @@
                 term = summed[64 * c + 8 * i : 64 * c + 8 * i + 8] * weights[0][i : i + 1]
                 total = term if total is None else total + term
             results.append(jnp.sum(total * weights[1], axis=0, keepdims=True))
-        out_ref[0, :, at : at + chunk] = jnp.concatenate(results, axis=0)
-
-
-def interpolate(points, table):
-    peers, _, slots = points.shape
+        store(slice(at, at + chunk), jnp.concatenate(results, axis=0))
+
+
+def exchange_kernel(
+    outer, inner, elems, chunk, send_ref, table_ref, const_ref, out_ref,
+    stacked, arrived, replies, landed, go_out, go_in, back_out, back_in,
+):
+    peers = outer * inner
+    slots = send_ref.shape[2]
+    my_x, my_y = lax.axis_index("gx"), lax.axis_index("gy")
+    me = my_x * inner + my_y
+
+    def after(s):
+        x, y = lax.rem(my_x + lax.rem(s, outer), outer), lax.rem(my_y + s // outer, inner)
+        return x, y, x * inner + y
+
+    def before(s):
+        x = lax.rem(my_x + outer - lax.rem(s, outer), outer)
+        y = lax.rem(my_y + inner - s // outer, inner)
+        return x, y, x * inner + y
+
+    barrier = pltpu.get_barrier_semaphore()
+
+    @pl.loop(1, peers)
+    def _(s):
+        x, y, _ = after(s)
+        pl.semaphore_signal(barrier, inc=1, device_id=(x, y), device_id_type=MESH)
+
+    hi, lo = split2(table_ref[...])
+    stacked[...] = jnp.concatenate([hi, hi, lo], axis=1).astype(BF16)
+    pl.semaphore_wait(barrier, peers - 1)
+
+    def outgoing(s):
+        x, y, target = after(s)
+        return pltpu.make_async_remote_copy(
+            src_ref=send_ref.at[target], dst_ref=arrived.at[me],
+            send_sem=go_out.at[target], recv_sem=go_in.at[me],
+            device_id=(x, y), device_id_type=MESH,
+        )
+
+    def incoming(s):
+        x, y, source = before(s)
+        return pltpu.make_async_remote_copy(
+            src_ref=send_ref.at[source], dst_ref=arrived.at[source],
+            send_sem=go_out.at[source], recv_sem=go_in.at[source],
+            device_id=(x, y), device_id_type=MESH,
+        )
+
+    def reply(s):
+        x, y, source = before(s)
+        return pltpu.make_async_remote_copy(
+            src_ref=replies.at[source], dst_ref=landed.at[me],
+            send_sem=back_out.at[source], recv_sem=back_in.at[me],
+            device_id=(x, y), device_id_type=MESH,
+        )
+
+    def answer(s):
+        x, y, target = after(s)
+        return pltpu.make_async_remote_copy(
+            src_ref=replies.at[target], dst_ref=landed.at[target],
+            send_sem=back_out.at[target], recv_sem=back_in.at[target],
+            device_id=(x, y), device_id_type=MESH,
+        )
+
+    @pl.loop(1, peers)
+    def _(s):
+        outgoing(s).start()
+
+    def own_store(where, value):
+        out_ref[me, :, where] = value
+
+    interp_chunks(elems, chunk, lambda where: send_ref[me, :, where], own_store, slots, stacked, const_ref)
+
+    @pl.loop(1, peers)
+    def _(s):
+        _, _, source = before(s)
+        incoming(s).wait_recv()
+
+        def store(where, value):
+            replies[source, :, where] = value
+
+        interp_chunks(elems, chunk, lambda where: arrived[source, :, where], store, slots, stacked, const_ref)
+
+        @pl.when(s > 1)
+        def _():
+            reply(s - 1).start()
+
+    @pl.loop(1, peers)
+    def _(s):
+        outgoing(s).wait_send()
+
+    reply(peers - 1).start()
+
+    @pl.loop(1, peers)
+    def _(s):
+        _, _, target = after(s)
+        answer(s).wait_recv()
+        out_ref[target] = landed[target]
+
+    @pl.loop(1, peers)
+    def _(s):
+        reply(s).wait_send()
+
+
+def exchange(send, table, outer, inner):
+    peers, _, slots = send.shape
     elems = table.shape[1] // 8
     chunk = math.gcd(slots, 256)
+    vmem = pl.BlockSpec(memory_space=pltpu.VMEM)
     return pl.pallas_call(
-        functools.partial(interp_kernel, elems, chunk),
-        grid=(peers,),
-        in_specs=[
-            pl.BlockSpec((1, 4, slots), lambda i: (i, 0, 0)),
-            pl.BlockSpec(table.shape, lambda i: (0, 0)),
-            pl.BlockSpec((8, 128), lambda i: (0, 0)),
-        ],
-        out_specs=pl.BlockSpec((1, 3, slots), lambda i: (i, 0, 0)),
+        functools.partial(exchange_kernel, outer, inner, elems, chunk),
+        in_specs=[vmem] * 3,
+        out_specs=vmem,
         out_shape=jax.ShapeDtypeStruct((peers, 3, slots), F32),
-        scratch_shapes=[pltpu.VMEM((192, 3 * table.shape[1]), BF16)],
-        compiler_params=pltpu.CompilerParams(dimension_semantics=("arbitrary",)),
-        name="interp",
-    )(points, table, jnp.asarray(lagrange_constants()))
-
-
-def pick_kernel(peers, per_step, answers_ref, owner_ref, slot_ref, select_ref, out_ref, faces_ref, halves):
+        scratch_shapes=[
+            pltpu.VMEM((192, 3 * table.shape[1]), BF16),
+            pltpu.VMEM((peers, 4, slots), F32),
+            pltpu.VMEM((peers, 3, slots), F32),
+            pltpu.VMEM((peers, 3, slots), F32),
+        ] + [pltpu.SemaphoreType.DMA((peers,))] * 4,
+        compiler_params=pltpu.CompilerParams(collective_id=0, has_side_effects=True),
+        name="exchange",
+    )(send, table, jnp.asarray(lagrange_constants()))
+
+
+def finish_kernel(
+    outer, inner, per_step, answers_ref, owner_ref, slot_ref, select_ref, index_ref, out_ref,
+    halves, faces, below, above, send_sem, recv_sem,
+):
     step = pl.program_id(0)
+    peers = outer * inner
     capacity = answers_ref.shape[2]
+    elems = out_ref.shape[1]
+    me = lax.axis_index("gx") * inner + lax.axis_index("gy")
+    up, down = lax.rem(me + 1, peers), lax.rem(me + peers - 1, peers)
+    barrier = pltpu.get_barrier_semaphore()
+
+    def place_of(device):
+        return (device // inner, lax.rem(device, inner))
 
     @pl.when(step == 0)
     def _():
+        for device in (up, down):
+            pl.semaphore_signal(barrier, inc=1, device_id=place_of(device), device_id_type=MESH)
         gap = jnp.zeros((1, capacity), F32)
         for p in range(0, peers, 2):
             rows = []
@@ -201,87 +311,82 @@
 
     @pl.when(step == pl.num_programs(0) - 1)
     def _():
+        sel = select_ref[...]
         for c in range(3):
             hi, lo = split2(out_ref[c])
             mid, low = split2(lo)
-            sel = select_ref[...]
-            faces_ref[c] = dot(hi.astype(BF16), sel) + dot(mid.astype(BF16), sel) + dot(low.astype(BF16), sel)
-
-
-def pick(answers, owner, slot, elems, select):
+            faces[c] = dot(hi.astype(BF16), sel) + dot(mid.astype(BF16), sel) + dot(low.astype(BF16), sel)
+        index = index_ref[...]
+        columns = lax.broadcasted_iota(jnp.int32, (6 * elems, 3 * elems), 1)
+        picker = (columns == index).astype(F32).astype(BF16)
+        present = (index >= 0).astype(F32)
+        pl.semaphore_wait(barrier, 2)
+        copies = [
+            pltpu.make_async_remote_copy(
+                src_ref=faces, dst_ref=land, send_sem=send_sem.at[k], recv_sem=recv_sem.at[k],
+                device_id=place_of(device), device_id_type=MESH,
+            )
+            for k, (device, land) in enumerate(((up, below), (down, above)))
+        ]
+        for copy in copies:
+            copy.start()
+        for copy in copies:
+            copy.wait()
+        for c in range(3):
+            own = faces[c]
+            extended = jnp.concatenate([below[c], own, above[c]], axis=0)
+            hi, lo = split2(extended)
+            across = dot(picker, hi.astype(BF16)) + dot(picker, lo.astype(BF16))
+            changes = []
+            for f in range(6):
+                g = f ^ 1
+                rows = slice(f * elems, (f + 1) * elems)
+                other = across[rows, 64 * g : 64 * g + 64]
+                changes.append(0.5 * (other - present[rows] * own[:, 64 * f : 64 * f + 64]))
+            hi, lo = split2(jnp.concatenate(changes, axis=1))
+            out_ref[c] += dot_nt(hi.astype(BF16), sel) + dot_nt(lo.astype(BF16), sel)
+
+
+def finish(answers, owner, slot, index, elems, outer, inner):
     peers, _, capacity = answers.shape
     points = owner.shape[1]
     per_step = math.gcd(elems, 2)
     block = per_step * 512
     return pl.pallas_call(
-        functools.partial(pick_kernel, peers, per_step),
+        functools.partial(finish_kernel, outer, inner, per_step),
         grid=(points // block,),
         in_specs=[
             pl.BlockSpec(answers.shape, lambda i: (0, 0, 0)),
             pl.BlockSpec((1, block), lambda i: (0, i)),
             pl.BlockSpec((1, block), lambda i: (0, i)),
             pl.BlockSpec((512, 384), lambda i: (0, 0)),
+            pl.BlockSpec(index.shape, lambda i: (0, 0)),
         ],
-        out_specs=[
-            pl.BlockSpec((3, elems, 512), lambda i: (0, 0, 0)),
-            pl.BlockSpec((3, elems, 384), lambda i: (0, 0, 0)),
-        ],
-        out_shape=[
-            jax.ShapeDtypeStruct((3, elems, 512), F32),
-            jax.ShapeDtypeStruct((3, elems, 384), F32),
-        ],
-        scratch_shapes=[pltpu.VMEM((8 * peers, capacity), BF16)],
-        compiler_params=pltpu.CompilerParams(dimension_semantics=("arbitrary",)),
-        name="pick",
-    )(answers, owner, slot, select)
-
-
-def faces_kernel(interp_ref, own_ref, prev_ref, next_ref, index_ref, select_ref, out_ref):
-    elems = interp_ref.shape[1]
-    index = index_ref[...]
-    columns = lax.broadcasted_iota(jnp.int32, (6 * elems, 3 * elems), 1)
-    picker = (columns == index).astype(F32).astype(BF16)
-    present = (index >= 0).astype(F32)
-    for c in range(3):
-        own = own_ref[c]
-        extended = jnp.concatenate([prev_ref[c], own, next_ref[c]], axis=0)
-        hi, lo = split2(extended)
-        across = dot(picker, hi.astype(BF16)) + dot(picker, lo.astype(BF16))
-        changes = []
-        for f in range(6):
-            g = f ^ 1
-            rows = slice(f * elems, (f + 1) * elems)
-            other = across[rows, 64 * g : 64 * g + 64]
-            changes.append(0.5 * (other - present[rows] * own[:, 64 * f : 64 * f + 64]))
-        hi, lo = split2(jnp.concatenate(changes, axis=1))
-        sel = select_ref[...]
-        out_ref[c] = interp_ref[c] + dot_nt(hi.astype(BF16), sel) + dot_nt(lo.astype(BF16), sel)
+        out_specs=pl.BlockSpec((3, elems, 512), lambda i: (0, 0, 0)),
+        out_shape=jax.ShapeDtypeStruct((3, elems, 512), F32),
+        scratch_shapes=[pltpu.VMEM((8 * peers, capacity), BF16)]
+        + [pltpu.VMEM((3, elems, 384), F32)] * 3
+        + [pltpu.SemaphoreType.DMA((2,))] * 2,
+        compiler_params=pltpu.CompilerParams(
+            dimension_semantics=("arbitrary",), collective_id=1, has_side_effects=True
+        ),
+        name="finish",
+    )(answers, owner, slot, jnp.asarray(face_selector(), BF16), index)
 
 
 def local(velocity, depart, owner_rank, owner_element_index, neighbours):
-    axes = ("gx", "gy")
-    inner_count = lax.axis_size("gy")
-    peers = lax.axis_size("gx") * inner_count
+    outer, inner = lax.axis_size("gx"), lax.axis_size("gy")
+    peers = outer * inner
     elems = velocity.shape[1]
     points = depart.shape[1]
     capacity = 2 * points // peers
     owner = owner_rank.reshape(1, points)
-    select = jnp.asarray(face_selector(), BF16)
+    table = velocity.reshape(3, elems, 64, 8).transpose(0, 2, 1, 3).reshape(192, elems * 8)
     send, slot = place(owner, depart, owner_element_index.reshape(1, points), peers, capacity)
-    received = lax.all_to_all(send, axes, split_axis=0, concat_axis=0, tiled=True)
-    table = velocity.reshape(3, elems, 64, 8).transpose(0, 2, 1, 3).reshape(192, elems * 8)
-    answers = interpolate(received, table)
-    answers = lax.all_to_all(answers, axes, split_axis=0, concat_axis=0, tiled=True)
-    interp, faces = pick(answers, owner, slot, elems, select)
-    before = lax.ppermute(faces, axes, [(i, i + 1) for i in range(peers - 1)])
-    after = lax.ppermute(faces, axes, [(i + 1, i) for i in range(peers - 1)])
-    device_id = lax.axis_index("gx") * inner_count + lax.axis_index("gy")
+    answers = exchange(send, table, outer, inner)
+    device_id = lax.axis_index("gx") * inner + lax.axis_index("gy")
     index = jnp.where(neighbours >= 0, neighbours - (device_id - 1) * elems, -1)
-    return pl.pallas_call(
-        faces_kernel,
-        out_shape=jax.ShapeDtypeStruct((3, elems, 512), F32),
-        name="faces",
-    )(interp, faces, before, after, index.reshape(6 * elems, 1), select)
+    return finish(answers, owner, slot, index.reshape(6 * elems, 1), elems, outer, inner)
 
 
 def solution(mesh):

time: 119 us -> 87.8 us (0.74); the launches traced: 116 us -> 87.6 us
  waiting for transfers between devices: 37.6 us -> 0 us
  Pallas kernels: 59.6 us -> 82.4 us
  starting transfers between devices: 14.1 us -> 0 us
    all_to_all x2 -> x0, waiting for transfers between devices: 30.4 us -> none  [the longest x1 16.2 us: local(): lax.all_to_all(answers, axes, split_axis=0, concat_axis=0, tiled=True)]
    pallas_call x3 -> x2, Pallas kernels: 42.1 us -> 64.9 us  [the longest x1 42 us: exchange(): pl.pallas_call(functools.partial(exchange_kernel, outer, inner, elems, ch...]
    all_to_all x2 -> x0, starting transfers between devices: 9.93 us -> none  [the longest x1 7.33 us: local(): lax.all_to_all(send, axes, split_axis=0, concat_axis=0, tiled=True)]
    ppermute x2 -> x0, waiting for transfers between devices: 7.19 us -> none  [the longest x1 5.59 us: local(): after = lax.ppermute(faces, axes, [(i + 1, i) for i in range(peers - 1)])]
    ppermute x2 -> x0, starting transfers between devices: 4.12 us -> none  [the longest x1 2.83 us: local(): before = lax.ppermute(faces, axes, [(i, i + 1) for i in range(peers - 1)])]
    unnamed x13 -> x6, local copies, waits for them, and re-layouts: 2.52 us -> 2.56 us
  transfers between devices with their start and end apart: 4 -> 0, of which waited for: 4 -> 0; matrix products, arithmetic and copies ran while one was open for 2% -> 0% of each run, Pallas kernels for 0% -> 0%
where the time goes in v2:
time: 87.8 us; the launch traced here: 87.6 us
  Pallas kernels  82.4 us (94%)
  local copies, waits for them, and re-layouts  5.09 us (6%)
    pallas_call x1, Pallas kernels, exchange(): pl.pallas_call(functools.partial(exchange_kernel, outer, inner, elems, ch...  42 us
    pallas_call x1, Pallas kernels, finish(): pl.pallas_call(functools.partial(finish_kernel, outer, inner, per_step),...  22.8 us
    pallas_call x1, Pallas kernels, place(): pl.pallas_call(functools.partial(place_kernel, peers, capacity, sub), gri...  17.6 us
    unnamed x6, local copies, waits for them, and re-layouts  2.56 us

profile of v2, /device:TPU:0, one launch (start us, length us, event | category | flops | bytes accessed | tf_op | source)
XLA Modules:
  0.0 87.6 jit_solution(18216073398625579216)
XLA Ops:
  0.0 0.0 copy-start
  0.0 17.6 %place.1 = (f32[32,4,1024]{2,1,0:T(4,128)}, s32[1,16384]{1,0:T(1,128)}) custom-call(s32[1,16384]{1,0:T(1,128)} %bitcast.8, f32[3,16384]{1,0:T(4,128)} %coords_ref.1, s32[1,16384]{1,0:T(1,128)} %bitcast.10, bf16[256,256]{1,0:T(8,128)(2,1)} %constant.24.clone.upper_ref), custom_call_target="tpu_custom_call" | custom-call | tf_op jit(solution)/shard_map/place/pallas_call | solution.py:101
  17.6 0.0 copy-done
  17.6 0.3 copy.10
  17.9 0.7 copy.11
  18.5 0.3 reshape.18
  18.9 0.8 copy.12.table_ref
  19.7 42.0 %exchange.1.answers_ref = f32[32,3,1024]{2,1,0:T(4,128)} custom-call(f32[32,4,1024]{2,1,0:T(4,128)} %get-tuple-element.7.send_ref, f32[192,256]{1,0:T(8,128)} %copy.12.table_ref, f32[8,128]{1,0:T(8,128)} %constant.25.clone.const_ref), custom_call_target="tpu_custom_call" | custom-call | tf_op jit(solution)/shard_map/exchange/pallas_call | solution.py:256
  61.7 0.0 copy-start.1
  61.7 0.7 copy-done.1
  62.4 0.8 reshape.20.index_ref
  63.1 22.8 %finish.1 = f32[3,32,512]{2,1,0:T(8,128)} custom-call(f32[32,3,1024]{2,1,0:T(4,128)} %exchange.1.answers_ref, s32[1,16384]{1,0:T(1,128)} %bitcast.9, s32[1,16384]{1,0:T(1,128)} %get-tuple-element.8.slot_ref, bf16[512,384]{1,0:T(8,128)(2,1)} %constant.26.clone.select_ref, s32[192,1]{1,0:T(8,128)} %reshape.20.index_ref), custom_call_target="tpu_custom_call" | custom-call | tf_op jit(solution)/shard_map/finish/pallas_call | solution.py:355
  86.0 1.6 %copy.15 = f32[3,32,512]{2,1,0:T(8,128)} copy(f32[3,32,512]{2,1,0:T(8,128)} %finish.1) | data formatting | bytes 393216
  (1 shorter events, 0.0 us)
Async XLA Ops:
  0.0 17.6 %copy-start = (f32[3,32,512]{2,1,0:T(8,128)S(1)}, f32[3,32,512]{2,1,0:T(8,128)}, u32[]{:S(2)}) copy-start(f32[3,32,512]{2,1,0:T(8,128)} %param.8) | copy-start | bytes 589828
  61.7 0.7 copy-start.1

commit v3 on v2

--- a/solution.py
+++ b/solution.py
@@ -54,10 +54,17 @@
     return lax.dot_general(a, b, (((1,), (1,)), ((), ())), preferred_element_type=F32)
 
 
-def place_kernel(peers, capacity, sub, owner_ref, coords_ref, elem_ref, upper_ref, send_ref, slot_ref, acc, carry):
-    step = pl.program_id(0)
-
-    @pl.when(step == 0)
+def one_hot_rows(slot, capacity):
+    width = slot.shape[1]
+    rows = lax.broadcasted_iota(jnp.int32, (capacity, 128), 0).astype(jnp.int16)
+    rows = jnp.concatenate([rows] * (width // 128), axis=1)
+    slots = jnp.broadcast_to(slot, (16, width)).astype(jnp.int16)
+    slots = jnp.concatenate([slots] * (capacity // 16), axis=0)
+    return jnp.where(rows == slots, jnp.array(1, BF16), jnp.array(0, BF16))
+
+
+def place_step(peers, capacity, sub, owner_ref, coords_ref, elem_ref, upper_ref, slot_ref, acc, carry):
+    @pl.when(pl.program_id(0) == 0)
     def _():
         acc[...] = jnp.zeros_like(acc)
         carry[...] = jnp.zeros_like(carry)
@@ -81,44 +88,8 @@
     hi, lo = split2(coords_ref[...])
     values = jnp.concatenate([hi, elem_ref[...].astype(F32), lo, jnp.zeros((1, block), F32)], axis=0)
     spread = jnp.concatenate([jnp.where(owner == p, values, 0.0) for p in range(peers)], axis=0).astype(BF16)
-    for at in range(0, capacity, 256):
-        width = min(256, capacity - at)
-        rows = lax.broadcasted_iota(jnp.int32, (width, block), 0) + at
-        hot = (rows == slot).astype(F32).astype(BF16)
-        acc[:, at : at + width] += dot_nt(spread, hot)
-
-    @pl.when(step == pl.num_programs(0) - 1)
-    def _():
-        for p in range(peers):
-            both = acc[8 * p : 8 * p + 8]
-            send_ref[p] = jnp.concatenate([both[0:3] + both[4:7], both[3:4]], axis=0)
-
-
-def place(owner, coords, elem, peers, capacity):
-    points = owner.shape[1]
-    block, sub = math.gcd(points, 1024), math.gcd(points, 256)
-    upper = np.triu(np.ones((sub, sub), np.float32), 1)
-    return pl.pallas_call(
-        functools.partial(place_kernel, peers, capacity, sub),
-        grid=(points // block,),
-        in_specs=[
-            pl.BlockSpec((1, block), lambda i: (0, i)),
-            pl.BlockSpec((3, block), lambda i: (0, i)),
-            pl.BlockSpec((1, block), lambda i: (0, i)),
-            pl.BlockSpec((sub, sub), lambda i: (0, 0)),
-        ],
-        out_specs=[
-            pl.BlockSpec((peers, 4, capacity), lambda i: (0, 0, 0)),
-            pl.BlockSpec((1, block), lambda i: (0, i)),
-        ],
-        out_shape=[
-            jax.ShapeDtypeStruct((peers, 4, capacity), F32),
-            jax.ShapeDtypeStruct((1, points), jnp.int32),
-        ],
-        scratch_shapes=[pltpu.VMEM((8 * peers, capacity), F32), pltpu.VMEM((peers, 128), F32)],
-        compiler_params=pltpu.CompilerParams(dimension_semantics=("arbitrary",)),
-        name="place",
-    )(owner, coords, elem, jnp.asarray(upper, BF16))
+    rows = lax.broadcasted_iota(jnp.int32, (capacity, block), 0)
+    acc[...] += dot_nt((rows == slot).astype(F32).astype(BF16), spread)
 
 
 def interp_chunks(elems, chunk, load, store, slots, stacked, const_ref):
@@ -148,11 +119,11 @@
 
 
 def exchange_kernel(
-    outer, inner, elems, chunk, send_ref, table_ref, const_ref, out_ref,
-    stacked, arrived, replies, landed, go_out, go_in, back_out, back_in,
+    outer, inner, elems, chunk, sub, owner_ref, coords_ref, elem_ref, upper_ref, table_ref, const_ref,
+    out_ref, slot_ref, acc, carry, send_ref, stacked, arrived, replies, landed, go_out, go_in, back_out, back_in,
 ):
     peers = outer * inner
-    slots = send_ref.shape[2]
+    slots = out_ref.shape[2]
     my_x, my_y = lax.axis_index("gx"), lax.axis_index("gy")
     me = my_x * inner + my_y
 
@@ -167,14 +138,17 @@
 
     barrier = pltpu.get_barrier_semaphore()
 
-    @pl.loop(1, peers)
-    def _(s):
-        x, y, _ = after(s)
-        pl.semaphore_signal(barrier, inc=1, device_id=(x, y), device_id_type=MESH)
-
-    hi, lo = split2(table_ref[...])
-    stacked[...] = jnp.concatenate([hi, hi, lo], axis=1).astype(BF16)
-    pl.semaphore_wait(barrier, peers - 1)
+    @pl.when(pl.program_id(0) == 0)
+    def _():
+        @pl.loop(1, peers)
+        def _(s):
+            x, y, _ = after(s)
+            pl.semaphore_signal(barrier, inc=1, device_id=(x, y), device_id_type=MESH)
+
+        hi, lo = split2(table_ref[...])
+        stacked[...] = jnp.concatenate([hi, hi, lo], axis=1).astype(BF16)
+
+    place_step(peers, slots, sub, owner_ref, coords_ref, elem_ref, upper_ref, slot_ref, acc, carry)
 
     def outgoing(s):
         x, y, target = after(s)
@@ -208,65 +182,95 @@
             device_id=(x, y), device_id_type=MESH,
         )
 
-    @pl.loop(1, peers)
-    def _(s):
-        outgoing(s).start()
-
-    def own_store(where, value):
-        out_ref[me, :, where] = value
-
-    interp_chunks(elems, chunk, lambda where: send_ref[me, :, where], own_store, slots, stacked, const_ref)
-
-    @pl.loop(1, peers)
-    def _(s):
-        _, _, source = before(s)
-        incoming(s).wait_recv()
-
-        def store(where, value):
-            replies[source, :, where] = value
-
-        interp_chunks(elems, chunk, lambda where: arrived[source, :, where], store, slots, stacked, const_ref)
-
-        @pl.when(s > 1)
-        def _():
-            reply(s - 1).start()
-
-    @pl.loop(1, peers)
-    def _(s):
-        outgoing(s).wait_send()
-
-    reply(peers - 1).start()
-
-    @pl.loop(1, peers)
-    def _(s):
-        _, _, target = after(s)
-        answer(s).wait_recv()
-        out_ref[target] = landed[target]
-
-    @pl.loop(1, peers)
-    def _(s):
-        reply(s).wait_send()
-
-
-def exchange(send, table, outer, inner):
-    peers, _, slots = send.shape
+    @pl.when(pl.program_id(0) == pl.num_programs(0) - 1)
+    def _():
+        turned = acc[...].T
+        for p in range(peers):
+            both = turned[8 * p : 8 * p + 8]
+            send_ref[p] = jnp.concatenate([both[0:3] + both[4:7], both[3:4]], axis=0)
+        pl.semaphore_wait(barrier, peers - 1)
+
+        @pl.loop(1, peers)
+        def _(s):
+            outgoing(s).start()
+
+        def own_store(where, value):
+            out_ref[me, :, where] = value
+
+        interp_chunks(elems, chunk, lambda where: send_ref[me, :, where], own_store, slots, stacked, const_ref)
+
+        @pl.loop(1, peers)
+        def _(s):
+            _, _, source = before(s)
+            incoming(s).wait_recv()
+
+            def store(where, value):
+                replies[source, :, where] = value
+
+            interp_chunks(elems, chunk, lambda where: arrived[source, :, where], store, slots, stacked, const_ref)
+
+            @pl.when(s > 1)
+            def _():
+                reply(s - 1).start()
+
+        @pl.loop(1, peers)
+        def _(s):
+            outgoing(s).wait_send()
+
+        reply(peers - 1).start()
+
+        @pl.loop(1, peers)
+        def _(s):
+            _, _, target = after(s)
+            answer(s).wait_recv()
+            out_ref[target] = landed[target]
+
+        @pl.loop(1, peers)
+        def _(s):
+            reply(s).wait_send()
+
+
+def exchange(owner, coords, elem, table, outer, inner, capacity):
+    peers = outer * inner
+    points = owner.shape[1]
     elems = table.shape[1] // 8
-    chunk = math.gcd(slots, 256)
-    vmem = pl.BlockSpec(memory_space=pltpu.VMEM)
+    chunk = math.gcd(capacity, 256)
+    block, sub = math.gcd(points, 4096), math.gcd(points, 256)
+    upper = np.triu(np.ones((sub, sub), np.float32), 1)
+    whole = lambda i: (0, 0)
     return pl.pallas_call(
-        functools.partial(exchange_kernel, outer, inner, elems, chunk),
-        in_specs=[vmem] * 3,
-        out_specs=vmem,
-        out_shape=jax.ShapeDtypeStruct((peers, 3, slots), F32),
+        functools.partial(exchange_kernel, outer, inner, elems, chunk, sub),
+        grid=(points // block,),
+        in_specs=[
+            pl.BlockSpec((1, block), lambda i: (0, i)),
+            pl.BlockSpec((3, block), lambda i: (0, i)),
+            pl.BlockSpec((1, block), lambda i: (0, i)),
+            pl.BlockSpec((sub, sub), whole),
+            pl.BlockSpec(table.shape, whole),
+            pl.BlockSpec((8, 128), whole),
+        ],
+        out_specs=[
+            pl.BlockSpec((peers, 3, capacity), lambda i: (0, 0, 0)),
+            pl.BlockSpec((1, block), lambda i: (0, i)),
+        ],
+        out_shape=[
+            jax.ShapeDtypeStruct((peers, 3, capacity), F32),
+            jax.ShapeDtypeStruct((1, points), jnp.int32),
+        ],
         scratch_shapes=[
+            pltpu.VMEM((capacity, 8 * peers), F32),
+            pltpu.VMEM((peers, 128), F32),
+            pltpu.VMEM((peers, 4, capacity), F32),
             pltpu.VMEM((192, 3 * table.shape[1]), BF16),
-            pltpu.VMEM((peers, 4, slots), F32),
-            pltpu.VMEM((peers, 3, slots), F32),
-            pltpu.VMEM((peers, 3, slots), F32),
+            pltpu.VMEM((peers, 4, capacity), F32),
+            pltpu.VMEM((peers, 3, capacity), F32),
+            pltpu.VMEM((peers, 3, capacity), F32),
         ] + [pltpu.SemaphoreType.DMA((peers,))] * 4,
-        compiler_params=pltpu.CompilerParams(collective_id=0, has_side_effects=True),
+        compiler_params=pltpu.CompilerParams(
+            dimension_semantics=("arbitrary",), collective_id=0, has_side_effects=True
+        ),
         name="exchange",
-    )(send, table, jnp.asarray(lagrange_constants()))
+    )(owner, coords, elem, jnp.asarray(upper, BF16), table, jnp.asarray(lagrange_constants()))
 
 
 def finish_kernel(
@@ -288,26 +292,19 @@
     def _():
         for device in (up, down):
             pl.semaphore_signal(barrier, inc=1, device_id=place_of(device), device_id_type=MESH)
-        gap = jnp.zeros((1, capacity), F32)
-        for p in range(0, peers, 2):
-            rows = []
-            for q in (p, p + 1):
-                hi, lo = split2(answers_ref[q])
-                rows += [hi, gap, lo, gap]
-            halves[8 * p : 8 * p + 16] = jnp.concatenate(rows, axis=0).astype(BF16)
+        for c in range(3):
+            hi, lo = split2(answers_ref[:, c, :])
+            halves[peers * c : peers * (c + 1)] = hi.astype(BF16)
+            halves[peers * (c + 3) : peers * (c + 4)] = lo.astype(BF16)
 
     for at in range(per_step):
         nodes = slice(512 * at, 512 * at + 512)
-        slot = slot_ref[:, nodes]
-        rows = lax.broadcasted_iota(jnp.int32, (capacity, 512), 0)
-        hot = (rows == slot).astype(F32).astype(BF16)
-        picked = dot(halves[...], hot)
-        owner = jnp.broadcast_to(owner_ref[:, nodes], (8, 512))
-        total = jnp.zeros((8, 512), F32)
-        for p in range(peers):
-            total = total + jnp.where(owner == p, picked[8 * p : 8 * p + 8], 0.0)
-        for c in range(3):
-            out_ref[c, pl.ds(step * per_step + at, 1), :] = total[c : c + 1] + total[c + 4 : c + 5]
+        picked = dot(halves[...], one_hot_rows(slot_ref[:, nodes], capacity))
+        match = lax.broadcasted_iota(jnp.int32, (peers, 512), 0) == owner_ref[:, nodes]
+        for c in range(3):
+            both = picked[peers * c : peers * (c + 1)] + picked[peers * (c + 3) : peers * (c + 4)]
+            value = jnp.sum(jnp.where(match, both, 0.0), axis=0, keepdims=True)
+            out_ref[c, pl.ds(step * per_step + at, 1), :] = value
 
     @pl.when(step == pl.num_programs(0) - 1)
     def _():
@@ -350,7 +347,7 @@
 def finish(answers, owner, slot, index, elems, outer, inner):
     peers, _, capacity = answers.shape
     points = owner.shape[1]
-    per_step = math.gcd(elems, 2)
+    per_step = math.gcd(elems, 8)
     block = per_step * 512
     return pl.pallas_call(
         functools.partial(finish_kernel, outer, inner, per_step),
@@ -364,7 +361,7 @@
         ],
         out_specs=pl.BlockSpec((3, elems, 512), lambda i: (0, 0, 0)),
         out_shape=jax.ShapeDtypeStruct((3, elems, 512), F32),
-        scratch_shapes=[pltpu.VMEM((8 * peers, capacity), BF16)]
+        scratch_shapes=[pltpu.VMEM((6 * peers, capacity), BF16)]
         + [pltpu.VMEM((3, elems, 384), F32)] * 3
         + [pltpu.SemaphoreType.DMA((2,))] * 2,
         compiler_params=pltpu.CompilerParams(
@@ -382,8 +379,8 @@
     capacity = 2 * points // peers
     owner = owner_rank.reshape(1, points)
     table = velocity.reshape(3, elems, 64, 8).transpose(0, 2, 1, 3).reshape(192, elems * 8)
-    send, slot = place(owner, depart, owner_element_index.reshape(1, points), peers, capacity)
-    answers = exchange(send, table, outer, inner)
+    elem = owner_element_index.reshape(1, points)
+    answers, slot = exchange(owner, depart, elem, table, outer, inner, capacity)
     device_id = lax.axis_index("gx") * inner + lax.axis_index("gy")
     index = jnp.where(neighbours >= 0, neighbours - (device_id - 1) * elems, -1)
     return finish(answers, owner, slot, index.reshape(6 * elems, 1), elems, outer, inner)

time: 87.8 us -> 75.3 us (0.86)
  Pallas kernels: 82.4 us -> 69 us
  local copies, waits for them, and re-layouts: 5.09 us -> 6.01 us
    pallas_call x1 -> x0, Pallas kernels: 17.6 us -> none  [place(): pl.pallas_call(functools.partial(place_kernel, peers, capacity, sub), gri...]
    pallas_call x1, Pallas kernels: 42 us -> 49.9 us  [exchange(): pl.pallas_call(functools.partial(exchange_kernel, outer, inner, elems, ch...]
    pallas_call x1, Pallas kernels: 22.8 us -> 19 us  [finish(): pl.pallas_call(functools.partial(finish_kernel, outer, inner, per_step),...]
    unnamed x6 -> x4, local copies, waits for them, and re-layouts: 2.56 us -> 3.48 us
where the time goes in v3:
time: 75.3 us; the launch traced here: 75 us
  Pallas kernels  69 us (92%)
  local copies, waits for them, and re-layouts  6.01 us (8%)
    pallas_call x1, Pallas kernels, exchange(): pl.pallas_call(functools.partial(exchange_kernel, outer, inner, elems, ch...  49.9 us
    pallas_call x1, Pallas kernels, finish(): pl.pallas_call(functools.partial(finish_kernel, outer, inner, per_step),...  19 us
    unnamed x4, local copies, waits for them, and re-layouts  3.48 us

profile of v3, /device:TPU:0, one launch (start us, length us, event | category | flops | bytes accessed | tf_op | source)
XLA Modules:
  0.0 75.0 jit_solution(5062923274428186492)
XLA Ops:
  0.0 1.2 %copy.10 = f32[3,32,512]{1,2,0:T(8,128)S(1)} copy(f32[3,32,512]{2,1,0:T(8,128)} %param.8) | data formatting | bytes 393216 | tf_op args[0]
  1.2 0.7 copy.11
  1.9 0.3 reshape.18
  2.2 0.8 %copy.12.table_ref = f32[192,256]{1,0:T(8,128)} copy(f32[192,256]{0,1:T(8,128)S(1)} %reshape.18) | data formatting | bytes 393216 | tf_op jit(solution)/shard_map/reshape | solution.py:381
  3.0 49.9 %exchange.1 = (f32[32,3,1024]{2,1,0:T(4,128)}, s32[1,16384]{1,0:T(1,128)}) custom-call(s32[1,16384]{1,0:T(1,128)} %bitcast.8, f32[3,16384]{1,0:T(4,128)} %coords_ref.1, s32[1,16384]{1,0:T(1,128)} %bitcast.10, bf16[256,256]{1,0:T(8,128)(2,1)} %constant.24.clone.upper_ref, f32[192,256]{1,0:T(8,128)} %copy.12.table_ref, f32[8,128]{1,0:T(8,128)} %constant.25.clone.const_ref), custom_call_target="tpu_custom_call" | custom-call | tf_op jit(solution)/shard_map/exchange/pallas_call | solution.py:241
  52.9 0.0 copy-start
  52.9 0.7 copy-done
  53.6 0.8 %reshape.20.index_ref = s32[192,1]{1,0:T(8,128)} reshape(s32[6,32]{1,0:T(8,128)S(1)} %subtract_select_fusion) | data formatting | bytes 1536 | tf_op jit(solution)/shard_map/reshape | solution.py:386
  54.4 19.0 %finish.1 = f32[3,32,512]{2,1,0:T(8,128)} custom-call(f32[32,3,1024]{2,1,0:T(4,128)} %get-tuple-element.7.answers_ref, s32[1,16384]{1,0:T(1,128)} %bitcast.9, s32[1,16384]{1,0:T(1,128)} %get-tuple-element.8.slot_ref, bf16[512,384]{1,0:T(8,128)(2,1)} %constant.26.clone.select_ref, s32[192,1]{1,0:T(8,128)} %reshape.20.index_ref), custom_call_target="tpu_custom_call" | custom-call | tf_op jit(solution)/shard_map/finish/pallas_call | solution.py:352
  73.4 1.6 %copy.15 = f32[3,32,512]{2,1,0:T(8,128)} copy(f32[3,32,512]{2,1,0:T(8,128)} %finish.1) | data formatting | bytes 393216
  (1 shorter events, 0.0 us)
Async XLA Ops:
  52.9 0.7 copy-start

commit v4 on v3

--- a/solution.py
+++ b/solution.py
@@ -309,27 +309,34 @@
     @pl.when(step == pl.num_programs(0) - 1)
     def _():
         sel = select_ref[...]
+        copies = [
+            [
+                pltpu.make_async_remote_copy(
+                    src_ref=faces.at[c], dst_ref=land.at[c],
+                    send_sem=send_sem.at[2 * c + k], recv_sem=recv_sem.at[2 * c + k],
+                    device_id=place_of(device), device_id_type=MESH,
+                )
+                for k, (device, land) in enumerate(((up, below), (down, above)))
+            ]
+            for c in range(3)
+        ]
+        pl.semaphore_wait(barrier, 2)
         for c in range(3):
             hi, lo = split2(out_ref[c])
             mid, low = split2(lo)
             faces[c] = dot(hi.astype(BF16), sel) + dot(mid.astype(BF16), sel) + dot(low.astype(BF16), sel)
+            if c > 0:
+                for copy in copies[c - 1]:
+                    copy.start()
         index = index_ref[...]
         columns = lax.broadcasted_iota(jnp.int32, (6 * elems, 3 * elems), 1)
         picker = (columns == index).astype(F32).astype(BF16)
         present = (index >= 0).astype(F32)
-        pl.semaphore_wait(barrier, 2)
-        copies = [
-            pltpu.make_async_remote_copy(
-                src_ref=faces, dst_ref=land, send_sem=send_sem.at[k], recv_sem=recv_sem.at[k],
-                device_id=place_of(device), device_id_type=MESH,
-            )
-            for k, (device, land) in enumerate(((up, below), (down, above)))
-        ]
-        for copy in copies:
+        for copy in copies[2]:
             copy.start()
-        for copy in copies:
-            copy.wait()
         for c in range(3):
+            for copy in copies[c]:
+                copy.wait()
             own = faces[c]
             extended = jnp.concatenate([below[c], own, above[c]], axis=0)
             hi, lo = split2(extended)
@@ -363,7 +370,7 @@
         out_shape=jax.ShapeDtypeStruct((3, elems, 512), F32),
         scratch_shapes=[pltpu.VMEM((6 * peers, capacity), BF16)]
         + [pltpu.VMEM((3, elems, 384), F32)] * 3
-        + [pltpu.SemaphoreType.DMA((2,))] * 2,
+        + [pltpu.SemaphoreType.DMA((6,))] * 2,
         compiler_params=pltpu.CompilerParams(
             dimension_semantics=("arbitrary",), collective_id=1, has_side_effects=True
         ),

time: 75.3 us -> 74.2 us (0.985)
  Pallas kernels: 69 us -> 67.9 us
    pallas_call x1, Pallas kernels: 19 us -> 18 us  [finish(): pl.pallas_call(functools.partial(finish_kernel, outer, inner, per_step),...]
where the time goes in v4:
time: 74.2 us; the launch traced here: 74 us
  Pallas kernels  67.9 us (92%)
  local copies, waits for them, and re-layouts  6.01 us (8%)
    pallas_call x1, Pallas kernels, exchange(): pl.pallas_call(functools.partial(exchange_kernel, outer, inner, elems, ch...  49.9 us
    pallas_call x1, Pallas kernels, finish(): pl.pallas_call(functools.partial(finish_kernel, outer, inner, per_step),...  18 us
    unnamed x4, local copies, waits for them, and re-layouts  3.48 us

profile of v4, /device:TPU:0, one launch (start us, length us, event | category | flops | bytes accessed | tf_op | source)
XLA Modules:
  0.0 74.0 jit_solution(5818291543025595679)
XLA Ops:
  0.0 1.2 %copy.10 = f32[3,32,512]{1,2,0:T(8,128)S(1)} copy(f32[3,32,512]{2,1,0:T(8,128)} %param.8) | data formatting | bytes 393216 | tf_op args[0]
  1.2 0.7 copy.11
  1.9 0.3 reshape.18
  2.2 0.8 %copy.12.table_ref = f32[192,256]{1,0:T(8,128)} copy(f32[192,256]{0,1:T(8,128)S(1)} %reshape.18) | data formatting | bytes 393216 | tf_op jit(solution)/shard_map/reshape | solution.py:388
  3.0 49.9 %exchange.1 = (f32[32,3,1024]{2,1,0:T(4,128)}, s32[1,16384]{1,0:T(1,128)}) custom-call(s32[1,16384]{1,0:T(1,128)} %bitcast.8, f32[3,16384]{1,0:T(4,128)} %coords_ref.1, s32[1,16384]{1,0:T(1,128)} %bitcast.10, bf16[256,256]{1,0:T(8,128)(2,1)} %constant.24.clone.upper_ref, f32[192,256]{1,0:T(8,128)} %copy.12.table_ref, f32[8,128]{1,0:T(8,128)} %constant.25.clone.const_ref), custom_call_target="tpu_custom_call" | custom-call | tf_op jit(solution)/shard_map/exchange/pallas_call | solution.py:241
  52.9 0.0 copy-start
  52.9 0.7 copy-done
  53.6 0.8 %reshape.20.index_ref = s32[192,1]{1,0:T(8,128)} reshape(s32[6,32]{1,0:T(8,128)S(1)} %subtract_select_fusion) | data formatting | bytes 1536 | tf_op jit(solution)/shard_map/reshape | solution.py:393
  54.4 18.0 %finish.1 = f32[3,32,512]{2,1,0:T(8,128)} custom-call(f32[32,3,1024]{2,1,0:T(4,128)} %get-tuple-element.7.answers_ref, s32[1,16384]{1,0:T(1,128)} %bitcast.9, s32[1,16384]{1,0:T(1,128)} %get-tuple-element.8.slot_ref, bf16[512,384]{1,0:T(8,128)(2,1)} %constant.26.clone.select_ref, s32[192,1]{1,0:T(8,128)} %reshape.20.index_ref), custom_call_target="tpu_custom_call" | custom-call | tf_op jit(solution)/shard_map/finish/pallas_call | solution.py:359
  72.4 1.6 %copy.15 = f32[3,32,512]{2,1,0:T(8,128)} copy(f32[3,32,512]{2,1,0:T(8,128)} %finish.1) | data formatting | bytes 393216
  (1 shorter events, 0.0 us)
Async XLA Ops:
  52.9 0.7 copy-start
